TPU v7x, 32 devices: a whole 2x2x4 slice. The times are simulated.
32 devices in a mesh: dp: 16 (over z, y, core), fsdp: 2 (over x).
Axes of the slice: x: 2, y: 2, z: 4, core: 2. Of those that a mesh axis runs over, the one named last changes fastest.
Arguments:
- hidden_in: bfloat16 [4096, 1024], P(('dp', 'fsdp')), may hold values from -6 to 6
- doc_id: int32 [4096], P(('dp', 'fsdp')), may hold values from 0 to 128, as said below
- expert_ids: int32 [4096, 8], P(('dp', 'fsdp')), may hold values from 0 to 15, all different within a row
- out_grad: bfloat16 [4096, 1024], P(('dp', 'fsdp')), may hold values from -6 to 6
- attn_gain: bfloat16 [1024], P(('dp', 'fsdp')), may hold values from 0.5 to 1.5
- query_weight: bfloat16 [1024, 1024], P(('dp', 'fsdp')), may hold values from -0.1875 to 0.1875
- key_weight: bfloat16 [1024, 512], P(('dp', 'fsdp')), may hold values from -0.1875 to 0.1875
- value_weight: bfloat16 [1024, 512], P(('dp', 'fsdp')), may hold values from -0.1875 to 0.1875
- output_weight: bfloat16 [1024, 1024], P(('dp', 'fsdp')), may hold values from -0.75 to 0.75
- ffn_gain: bfloat16 [1024], P(('dp', 'fsdp')), may hold values from 0.5 to 1.5
- router_weight: bfloat16 [1024, 16], P(('dp', 'fsdp')), may hold values from -0.375 to 0.375
- expert_gate: bfloat16 [16, 1024, 512], P('dp', 'fsdp'), may hold values from -0.1875 to 0.1875
- expert_up: bfloat16 [16, 1024, 512], P('dp', 'fsdp'), may hold values from -0.1875 to 0.1875
- expert_down: bfloat16 [16, 512, 1024], P('dp', 'fsdp'), may hold values from -1 to 1
Outputs:
- layer_out: bfloat16 [4096, 1024], P(('dp', 'fsdp'))
- grad_in: bfloat16 [4096, 1024], P(('dp', 'fsdp'))
- grad_attn_gain: float32 [1024], P(('dp', 'fsdp'))
- grad_query: float32 [1024, 1024], P(('dp', 'fsdp'))
- grad_key: float32 [1024, 512], P(('dp', 'fsdp'))
- grad_value: float32 [1024, 512], P(('dp', 'fsdp'))
- grad_output: float32 [1024, 1024], P(('dp', 'fsdp'))
- grad_ffn_gain: float32 [1024], P(('dp', 'fsdp'))
- grad_router: float32 [1024, 16], P(('dp', 'fsdp'))
- grad_expert_gate: float32 [16, 1024, 512], P('dp', 'fsdp')
- grad_expert_up: float32 [16, 1024, 512], P('dp', 'fsdp')
- grad_expert_down: float32 [16, 512, 1024], P('dp', 'fsdp')
Inputs may be any that keep to these rules, and one draw needn't show every extreme that they name: Within each block of 128 rows doc_id starts at 0 and never falls; live rows come first and carry ids below 128; the rows after them carry 128 (padding). Every block has 64 or more live rows and some block has no padding. `expert_ids`: each row names 8 different experts.
All inputs are finite; a program needn't handle non-finite values.
Results may differ from a plain program's by a relative error of at most 0.015.
The roundings to bfloat16 on the way count: a program that leaves them out, or rounds other values in their place, can miss the bound.
Values may be sent and summed in bfloat16 or wider, within the bound.
A program may use at most 128 MiB of HBM per device.

v0:
```python
import jax
import jax.numpy as jnp
from jax import lax
from jax.sharding import PartitionSpec as P

HEADS = 16
KV_HEADS = 8
HEAD_DIM = 64
TOP = 8
CAP = 24


norm_eps = 1e-05


def positions_mask(doc_block):
    row_count = doc_block.shape[0]
    row_index = jnp.arange(row_count)
    same_doc = doc_block[:, None] == doc_block[None, :]
    earlier = row_index[None, :] < row_index[:, None]
    position = jnp.sum((same_doc & earlier).astype(jnp.float32), axis=1)
    allowed = same_doc & (row_index[None, :] <= row_index[:, None])
    live_rows = (doc_block < row_count).astype(jnp.float32)
    return (position, allowed, live_rows)


def rope_tables(position):
    half_dim = HEAD_DIM // 2
    freqs = jnp.exp(-jnp.log(10000.0) * (2.0 * jnp.arange(half_dim, dtype=jnp.float32) / HEAD_DIM))
    angle = position[:, None] * freqs[None, :]
    return (jnp.cos(angle), jnp.sin(angle))


def rotate(values, cosine, sinusoid):
    half_dim = values.shape[-1] // 2
    first_half, second_half = (values[..., :half_dim], values[..., half_dim:])
    return jnp.concatenate(
        [
            first_half * cosine - second_half * sinusoid,
            second_half * cosine + first_half * sinusoid,
        ],
        axis=-1,
    )


def unrotate(values, cosine, sinusoid):
    half_dim = values.shape[-1] // 2
    first_half, second_half = (values[..., :half_dim], values[..., half_dim:])
    return jnp.concatenate(
        [
            first_half * cosine + second_half * sinusoid,
            second_half * cosine - first_half * sinusoid,
        ],
        axis=-1,
    )


def norm_forward(values, gain):
    scale_row = lax.rsqrt(jnp.mean(values * values, axis=-1, keepdims=True) + norm_eps)
    normed = values * scale_row
    return (normed, scale_row, (normed * gain).astype(jnp.bfloat16))


def norm_backward(upstream, normed, scale_row, gain):
    scaled = upstream * gain
    inner = jnp.mean(scaled * normed, axis=-1, keepdims=True)
    return (scale_row * (scaled - normed * inner), jnp.sum(upstream * normed, axis=0))


def probabilities(query_b, key_b, allowed, log_total):
    scores = jnp.einsum(
        "ikgd,jkd->kgij", query_b, key_b, preferred_element_type=jnp.float32
    ) * HEAD_DIM ** (-0.5)
    raised = jnp.where(allowed[None, None], jnp.exp(scores), 0.0)
    if log_total is None:
        log_total = jnp.log(jnp.sum(raised, axis=-1, keepdims=True))
    return (jnp.where(allowed[None, None], jnp.exp(scores - log_total), 0.0), log_total)


def routing(expert_block, live_rows, logits):
    experts = logits.shape[1]
    row_count = expert_block.shape[0]
    chosen = jnp.sum(
        (expert_block[:, :, None] == jnp.arange(experts)[None, None, :]).astype(jnp.float32), axis=1
    )
    raised = jnp.where(chosen > 0, jnp.exp(logits), 0.0)
    gates = raised / jnp.sum(raised, axis=1, keepdims=True)
    member = chosen * live_rows[:, None]
    lower = (jnp.arange(row_count)[None, :] < jnp.arange(row_count)[:, None]).astype(jnp.float32)
    rank = jnp.dot(lower, member, precision=lax.Precision.HIGHEST)
    kept = member * (rank < CAP).astype(jnp.float32)
    slot_match = (rank.T[:, None, :] == jnp.arange(CAP, dtype=jnp.float32)[None, :, None]).astype(
        jnp.float32
    )
    dispatch = kept.T[:, None, :] * slot_match
    return (gates, dispatch, kept, rank)


def expert_forward(rows_in, w_gate, w_up, w_down):
    gate_pre = jnp.dot(rows_in, w_gate, preferred_element_type=jnp.float32)
    up_pre = jnp.dot(rows_in, w_up, preferred_element_type=jnp.float32)
    act_rows = (jax.nn.silu(gate_pre) * up_pre).astype(jnp.bfloat16)
    out_rows = jnp.dot(act_rows, w_down, preferred_element_type=jnp.float32).astype(jnp.bfloat16)
    return (gate_pre, up_pre, act_rows, out_rows)


def expert_backward(rows_in, gate_pre, up_pre, act_rows, grad_rows, w_gate, w_up, w_down):
    grad_act = jnp.dot(grad_rows, w_down.T, preferred_element_type=jnp.float32)
    sigmoid_gate = jax.nn.sigmoid(gate_pre)
    grad_up_pre = (grad_act * gate_pre * sigmoid_gate).astype(jnp.bfloat16)
    grad_gate_pre = (
        grad_act * up_pre * sigmoid_gate * (1.0 + gate_pre * (1.0 - sigmoid_gate))
    ).astype(jnp.bfloat16)
    grad_down_w = jnp.dot(act_rows.T, grad_rows, preferred_element_type=jnp.float32)
    grad_gate_w = jnp.dot(rows_in.T, grad_gate_pre, preferred_element_type=jnp.float32)
    grad_up_w = jnp.dot(rows_in.T, grad_up_pre, preferred_element_type=jnp.float32)
    grad_rows_in = jnp.dot(grad_gate_pre, w_gate.T, preferred_element_type=jnp.float32)
    grad_rows_in = (
        grad_rows_in + jnp.dot(grad_up_pre, w_up.T, preferred_element_type=jnp.float32)
    ).astype(jnp.bfloat16)
    return (grad_rows_in, grad_gate_w, grad_up_w, grad_down_w)


def shards(
    hidden_in,
    doc_id,
    expert_ids,
    out_grad,
    attn_gain,
    query_weight,
    key_weight,
    value_weight,
    output_weight,
    ffn_gain,
    router_weight,
    expert_gate,
    expert_up,
    expert_down,
):
    rows = hidden_in.shape[0]
    groups = HEADS // KV_HEADS
    scale = HEAD_DIM ** (-0.5)
    dense_full = (
        lax.all_gather(attn_gain, ("dp", "fsdp"), axis=0, tiled=True),
        lax.all_gather(query_weight, ("dp", "fsdp"), axis=0, tiled=True),
        lax.all_gather(key_weight, ("dp", "fsdp"), axis=0, tiled=True),
        lax.all_gather(value_weight, ("dp", "fsdp"), axis=0, tiled=True),
        lax.all_gather(output_weight, ("dp", "fsdp"), axis=0, tiled=True),
        lax.all_gather(ffn_gain, ("dp", "fsdp"), axis=0, tiled=True),
        lax.all_gather(router_weight, ("dp", "fsdp"), axis=0, tiled=True),
    )
    expert_full = (
        lax.all_gather(expert_gate, "fsdp", axis=1, tiled=True),
        lax.all_gather(expert_up, "fsdp", axis=1, tiled=True),
        lax.all_gather(expert_down, "fsdp", axis=1, tiled=True),
    )
    gain_one, w_query, w_key, w_value, w_output, gain_two, w_router = dense_full
    w_gate, w_up, w_down = (expert_full[0][0], expert_full[1][0], expert_full[2][0])
    position, allowed, live_rows = positions_mask(doc_id)
    cosine, sinusoid = rope_tables(position)
    cos_query, sin_query = (cosine[:, None, None, :], sinusoid[:, None, None, :])
    cos_key, sin_key = (cosine[:, None, :], sinusoid[:, None, :])
    resid_in = hidden_in.astype(jnp.float32)
    normed_one, scale_one, normed_in = norm_forward(resid_in, gain_one.astype(jnp.float32))
    query_raw = jnp.dot(normed_in, w_query, preferred_element_type=jnp.float32).reshape(
        rows, KV_HEADS, groups, HEAD_DIM
    )
    key_raw = jnp.dot(normed_in, w_key, preferred_element_type=jnp.float32).reshape(
        rows, KV_HEADS, HEAD_DIM
    )
    query_b = rotate(query_raw, cos_query, sin_query).astype(jnp.bfloat16)
    key_b = rotate(key_raw, cos_key, sin_key).astype(jnp.bfloat16)
    value_b = (
        jnp.dot(normed_in, w_value, preferred_element_type=jnp.float32)
        .reshape(rows, KV_HEADS, HEAD_DIM)
        .astype(jnp.bfloat16)
    )
    probs, log_total = probabilities(query_b, key_b, allowed, None)
    probs_b = probs.astype(jnp.bfloat16)
    mixed = jnp.einsum("kgij,jkd->ikgd", probs_b, value_b, preferred_element_type=jnp.float32)
    mixed_b = (
        (mixed * live_rows[:, None, None, None])
        .reshape(rows, HEADS * HEAD_DIM)
        .astype(jnp.bfloat16)
    )
    resid_mid = resid_in + jnp.dot(mixed_b, w_output, preferred_element_type=jnp.float32)
    normed_two, scale_two, routed_in = norm_forward(resid_mid, gain_two.astype(jnp.float32))
    logits = jnp.dot(routed_in, w_router, preferred_element_type=jnp.float32)
    gates, dispatch, kept, rank = routing(expert_ids, live_rows, logits)
    dispatch_b = dispatch.astype(jnp.bfloat16)
    send_rows = jnp.einsum(
        "ecr,rd->ecd", dispatch_b, routed_in, preferred_element_type=jnp.float32
    ).astype(jnp.bfloat16)
    recv_rows = lax.all_to_all(send_rows, "dp", split_axis=0, concat_axis=0, tiled=True)
    flat_in = recv_rows.reshape(-1, recv_rows.shape[2])
    gate_pre, up_pre, act_rows, out_rows = expert_forward(flat_in, w_gate, w_up, w_down)
    back_rows = lax.all_to_all(
        out_rows.reshape(recv_rows.shape), "dp", split_axis=0, concat_axis=0, tiled=True
    )
    experts = back_rows.shape[0]
    capacity = back_rows.shape[1]
    width = back_rows.shape[2]
    chosen_slot = (expert_ids[:, :, None] == jnp.arange(experts)[None, None, :]).astype(jnp.float32)
    gate_pick = jnp.sum(chosen_slot * (gates * kept)[:, None, :], axis=2)
    rank_pick = jnp.sum(chosen_slot * rank[:, None, :], axis=2)
    slot_index = expert_ids * capacity + jnp.minimum(rank_pick, capacity - 1.0).astype(jnp.int32)
    back_flat = back_rows.reshape(experts * capacity, width)
    picked_rows = jnp.take(back_flat, slot_index.reshape(-1), axis=0).reshape(rows, TOP, width)
    expert_sum = jnp.sum(gate_pick[:, :, None] * picked_rows.astype(jnp.float32), axis=1)
    layer_out = (resid_mid + expert_sum).astype(jnp.bfloat16)
    dense_full = (
        lax.all_gather(attn_gain, ("dp", "fsdp"), axis=0, tiled=True),
        lax.all_gather(query_weight, ("dp", "fsdp"), axis=0, tiled=True),
        lax.all_gather(key_weight, ("dp", "fsdp"), axis=0, tiled=True),
        lax.all_gather(value_weight, ("dp", "fsdp"), axis=0, tiled=True),
        lax.all_gather(output_weight, ("dp", "fsdp"), axis=0, tiled=True),
        lax.all_gather(ffn_gain, ("dp", "fsdp"), axis=0, tiled=True),
        lax.all_gather(router_weight, ("dp", "fsdp"), axis=0, tiled=True),
    )
    expert_full = (
        lax.all_gather(expert_gate, "fsdp", axis=1, tiled=True),
        lax.all_gather(expert_up, "fsdp", axis=1, tiled=True),
        lax.all_gather(expert_down, "fsdp", axis=1, tiled=True),
    )
    gain_one, w_query, w_key, w_value, w_output, gain_two, w_router = dense_full
    w_gate, w_up, w_down = (expert_full[0][0], expert_full[1][0], expert_full[2][0])
    grad_out = out_grad.astype(jnp.float32)
    slot_gate = jnp.sum(dispatch * gates.T[:, None, :], axis=2)
    pulled_grad = jnp.einsum(
        "ecr,rd->ecd", dispatch_b, out_grad, preferred_element_type=jnp.float32
    )
    grad_send = (slot_gate[:, :, None] * pulled_grad).astype(jnp.bfloat16)
    slot_dot = jnp.sum(back_rows.astype(jnp.float32) * pulled_grad, axis=2)
    grad_gates = jnp.sum(dispatch * slot_dot[:, :, None], axis=1).T
    grad_logits = gates * (grad_gates - jnp.sum(gates * grad_gates, axis=1, keepdims=True))
    grad_logits_b = grad_logits.astype(jnp.bfloat16)
    grad_recv = lax.all_to_all(grad_send, "dp", split_axis=0, concat_axis=0, tiled=True)
    grad_rows_in, grad_gate_w, grad_up_w, grad_down_w = expert_backward(
        flat_in, gate_pre, up_pre, act_rows, grad_recv.reshape(flat_in.shape), w_gate, w_up, w_down
    )
    grad_back = lax.all_to_all(
        grad_rows_in.reshape(recv_rows.shape), "dp", split_axis=0, concat_axis=0, tiled=True
    )
    grad_routed = jnp.einsum(
        "ecr,ecd->rd", dispatch_b, grad_back, preferred_element_type=jnp.float32
    )
    grad_routed = grad_routed + jnp.dot(
        grad_logits_b, w_router.T, preferred_element_type=jnp.float32
    )
    grad_w_router = jnp.dot(routed_in.T, grad_logits_b, preferred_element_type=jnp.float32)
    grad_norm_two, grad_gain_two = norm_backward(
        grad_routed, normed_two, scale_two, gain_two.astype(jnp.float32)
    )
    grad_mid = grad_out + grad_norm_two
    grad_mid_b = grad_mid.astype(jnp.bfloat16)
    grad_w_output = jnp.dot(mixed_b.T, grad_mid_b, preferred_element_type=jnp.float32)
    grad_mixed = jnp.dot(grad_mid_b, w_output.T, preferred_element_type=jnp.float32).reshape(
        rows, KV_HEADS, groups, HEAD_DIM
    )
    grad_mixed = (grad_mixed * live_rows[:, None, None, None]).astype(jnp.bfloat16)
    probs_again, unused_total = probabilities(query_b, key_b, allowed, log_total)
    grad_probs = jnp.einsum(
        "ikgd,jkd->kgij", grad_mixed, value_b, preferred_element_type=jnp.float32
    )
    delta = jnp.sum(probs_again * grad_probs, axis=-1, keepdims=True)
    grad_scores = (probs_again * (grad_probs - delta) * scale).astype(jnp.bfloat16)
    grad_query_raw = jnp.einsum(
        "kgij,jkd->ikgd", grad_scores, key_b, preferred_element_type=jnp.float32
    )
    grad_key_raw = jnp.einsum(
        "kgij,ikgd->jkd", grad_scores, query_b, preferred_element_type=jnp.float32
    )
    grad_value_raw = jnp.einsum(
        "kgij,ikgd->jkd",
        probs_again.astype(jnp.bfloat16),
        grad_mixed,
        preferred_element_type=jnp.float32,
    )
    grad_query_b = (
        unrotate(grad_query_raw, cos_query, sin_query)
        .reshape(rows, HEADS * HEAD_DIM)
        .astype(jnp.bfloat16)
    )
    grad_key_b = (
        unrotate(grad_key_raw, cos_key, sin_key)
        .reshape(rows, KV_HEADS * HEAD_DIM)
        .astype(jnp.bfloat16)
    )
    grad_value_b = grad_value_raw.reshape(rows, KV_HEADS * HEAD_DIM).astype(jnp.bfloat16)
    grad_w_query = jnp.dot(normed_in.T, grad_query_b, preferred_element_type=jnp.float32)
    grad_w_key = jnp.dot(normed_in.T, grad_key_b, preferred_element_type=jnp.float32)
    grad_w_value = jnp.dot(normed_in.T, grad_value_b, preferred_element_type=jnp.float32)
    grad_normed = jnp.dot(grad_query_b, w_query.T, preferred_element_type=jnp.float32)
    grad_normed = grad_normed + jnp.dot(grad_key_b, w_key.T, preferred_element_type=jnp.float32)
    grad_normed = grad_normed + jnp.dot(grad_value_b, w_value.T, preferred_element_type=jnp.float32)
    grad_norm_one, grad_gain_one = norm_backward(
        grad_normed, normed_one, scale_one, gain_one.astype(jnp.float32)
    )
    grad_input = (grad_mid + grad_norm_one).astype(jnp.bfloat16)
    dense_grads = (
        lax.psum_scatter(grad_gain_one, ("dp", "fsdp"), scatter_dimension=0, tiled=True),
        lax.psum_scatter(grad_w_query, ("dp", "fsdp"), scatter_dimension=0, tiled=True),
        lax.psum_scatter(grad_w_key, ("dp", "fsdp"), scatter_dimension=0, tiled=True),
        lax.psum_scatter(grad_w_value, ("dp", "fsdp"), scatter_dimension=0, tiled=True),
        lax.psum_scatter(grad_w_output, ("dp", "fsdp"), scatter_dimension=0, tiled=True),
        lax.psum_scatter(grad_gain_two, ("dp", "fsdp"), scatter_dimension=0, tiled=True),
        lax.psum_scatter(grad_w_router, ("dp", "fsdp"), scatter_dimension=0, tiled=True),
    )
    expert_grads = (
        lax.psum_scatter(
            grad_gate_w[None].astype(jnp.bfloat16), "fsdp", scatter_dimension=1, tiled=True
        ).astype(jnp.float32),
        lax.psum_scatter(
            grad_up_w[None].astype(jnp.bfloat16), "fsdp", scatter_dimension=1, tiled=True
        ).astype(jnp.float32),
        lax.psum_scatter(
            grad_down_w[None].astype(jnp.bfloat16), "fsdp", scatter_dimension=1, tiled=True
        ).astype(jnp.float32),
    )
    return (
        layer_out,
        grad_input,
        dense_grads[0],
        dense_grads[1],
        dense_grads[2],
        dense_grads[3],
        dense_grads[4],
        dense_grads[5],
        dense_grads[6],
        expert_grads[0],
        expert_grads[1],
        expert_grads[2],
    )


def solution(mesh):
    in_specs = (
        P(("dp", "fsdp"), None),
        P(("dp", "fsdp")),
        P(("dp", "fsdp"), None),
        P(("dp", "fsdp"), None),
        P(("dp", "fsdp")),
        P(("dp", "fsdp"), None),
        P(("dp", "fsdp"), None),
        P(("dp", "fsdp"), None),
        P(("dp", "fsdp"), None),
        P(("dp", "fsdp")),
        P(("dp", "fsdp"), None),
        P("dp", "fsdp", None),
        P("dp", "fsdp", None),
        P("dp", "fsdp", None),
    )
    out_specs = (
        P(("dp", "fsdp"), None),
        P(("dp", "fsdp"), None),
        P(("dp", "fsdp")),
        P(("dp", "fsdp"), None),
        P(("dp", "fsdp"), None),
        P(("dp", "fsdp"), None),
        P(("dp", "fsdp"), None),
        P(("dp", "fsdp")),
        P(("dp", "fsdp"), None),
        P("dp", "fsdp", None),
        P("dp", "fsdp", None),
        P("dp", "fsdp", None),
    )
    return jax.shard_map(shards, mesh=mesh, in_specs=in_specs, out_specs=out_specs, check_vma=False)
```

profile of v0, /device:TPU:0, one launch (start us, length us, event | category | flops | bytes accessed | tf_op | source)
XLA Modules:
  0.0 1174.7 jit_solution(4902561280423588323)
XLA Ops:
  15.2 41.9 %all-reduce.5 = (bf16[1024]{0:T(1024)(128)(2,1)S(1)}, bf16[1024]{0:T(1024)(128)(2,1)S(1)}) all-reduce(bf16[1024]{0:T(1024)(128)(2,1)S(1)} %dynamic-update-slice, bf16[1024]{0:T(1024)(128)(2,1)S(1)} %dynamic-update-slice.1), channel_id=1, replica_groups=mesh['dp'=16,'fsdp'=2] {'dp','fsdp'}, use_global_device_ids=true, to_apply=%add | all-reduce | flops 2048 | bytes 8192
  59.3 8.2 all-gather.9.cloned.1.call-done
  69.3 54.0 %all-gather.11.cloned.1.call-done = bf16[1024,512]{1,0:T(8,128)(2,1)} async-done(((bf16[32,512]{1,0:T(8,128)(2,1)}), bf16[1024,512]{1,0:T(8,128)(2,1)}) %all-gather.11.cloned.1.call-update) | async-done | bytes 1048592 | tf_op jit(solution)/shard_map/all_gather | solution.py:146
  125.1 56.5 %all-gather.13.cloned.1.call-done = bf16[1024,1024]{1,0:T(8,128)(2,1)} async-done(((bf16[32,1024]{1,0:T(8,128)(2,1)}), bf16[1024,1024]{1,0:T(8,128)(2,1)}) %all-gather.13.cloned.1.call-update) | async-done | bytes 2097168 | tf_op jit(solution)/shard_map/all_gather | solution.py:145
  185.5 54.2 %all-gather.15.cloned.1.call-done = bf16[1024,1024]{1,0:T(8,128)(2,1)} async-done(((bf16[32,1024]{1,0:T(8,128)(2,1)}), bf16[1024,1024]{1,0:T(8,128)(2,1)}) %all-gather.15.cloned.1.call-update) | async-done | bytes 2097168 | tf_op jit(solution)/shard_map/all_gather | solution.py:148
  244.0 4.5 all-to-all-start
  249.2 12.0 %all-gather.17.cloned.1.call-done = bf16[1,1024,512]{2,1,0:T(8,128)(2,1)} async-done(((bf16[1,512,512]{2,1,0:T(8,128)(2,1)}), bf16[1,1024,512]{2,1,0:T(8,128)(2,1)}) %all-gather.17.cloned.1.call-update) | async-done | bytes 1048592 | tf_op jit(solution)/shard_map/all_gather | solution.py:153
  261.2 5.9 all-to-all-done
  268.9 15.0 %all-gather.19.cloned.1.call-done = bf16[1,1024,512]{2,1,0:T(8,128)(2,1)} async-done(((bf16[1,512,512]{2,1,0:T(8,128)(2,1)}), bf16[1,1024,512]{2,1,0:T(8,128)(2,1)}) %all-gather.19.cloned.1.call-update) | async-done | bytes 1048592 | tf_op jit(solution)/shard_map/all_gather | solution.py:154
  286.6 20.2 %all-gather.21.cloned.1.call-done = bf16[1,512,1024]{2,1,0:T(8,128)(2,1)} async-done(((bf16[1,256,1024]{2,1,0:T(8,128)(2,1)}), bf16[1,512,1024]{2,1,0:T(8,128)(2,1)}) %all-gather.21.cloned.1.call-update) | async-done | bytes 1048592 | tf_op jit(solution)/shard_map/all_gather | solution.py:155
  309.6 5.6 all-to-all-start.1
  315.2 76.2 %all-gather = bf16[32,32,16]{1,2,0:T(8,128)(2,1)S(1)} all-gather(bf16[1,32,16]{1,2,0:T(8,128)(2,1)S(1)} %bitcast.165), channel_id=1, replica_groups=mesh['dp'=16,'fsdp'=2] {'dp','fsdp'}, dimensions={0}, use_global_device_ids=true | all-gather | bytes 33792 | tf_op jit(solution)/shard_map/all_gather | solution.py:150
  393.6 3.6 all-to-all-start.2
  399.0 16.8 %all-to-all-done.2 = bf16[16,24,1024]{2,1,0:T(8,128)(2,1)S(1)} async-done(((bf16[16,24,1024]{2,1,0:T(8,128)(2,1)}), bf16[16,24,1024]{2,1,0:T(8,128)(2,1)S(1)}, u32[]{:S(2)}, u32[]{:S(2)}) %all-to-all-start.2) | async-done | bytes 786464 | tf_op jit(solution)/shard_map/all_to_all | solution.py:237
  426.2 5.7 all-to-all-start.3
  433.9 4.1 gather_fusion
  442.1 8.6 all-to-all-done.3
  472.3 65.3 %reduce-scatter.25.cloned.1.call-done = f32[32,16]{1,0:T(8,128)} async-done(((f32[1024,16]{1,0:T(8,128)}), f32[32,16]{1,0:T(8,128)}) %reduce-scatter.25.cloned.1.call-update) | async-done | bytes 2064
  541.4 38.1 %all-reduce.4 = (f32[1024]{0:T(1024)S(1)}, f32[1024]{0:T(1024)S(1)}) all-reduce(f32[1024]{0:T(1024)S(1)} %get-tuple-element.14, f32[1024]{0:T(1024)S(1)} %copy-done.49), channel_id=2, replica_groups=mesh['dp'=16,'fsdp'=2] {'dp','fsdp'}, use_global_device_ids=true, to_apply=%region_17.18.clone | all-reduce | flops 2048 | bytes 16384
  585.9 17.1 %reduce-scatter.23.cloned.1.call-done = bf16[1,256,1024]{2,1,0:T(8,128)(2,1)} async-done(((bf16[1,512,1024]{2,1,0:T(8,128)(2,1)}), bf16[1,256,1024]{2,1,0:T(8,128)(2,1)}) %reduce-scatter.23.cloned.1.call-update) | async-done | bytes 524304 | tf_op jit(solution)/shard_map/reduce_scatter | solution.py:316
  605.0 139.8 %reduce-scatter.13.cloned.1.call-done = f32[32,512]{1,0:T(8,128)} async-done(((f32[1024,512]{1,0:T(8,128)}), f32[32,512]{1,0:T(8,128)}) %reduce-scatter.13.cloned.1.call-update) | async-done | bytes 65552 | tf_op jit(solution)/shard_map/reduce_scatter | solution.py:303
  744.9 137.4 %reduce-scatter.15.cloned.1.call-done = f32[32,512]{1,0:T(8,128)} async-done(((f32[1024,512]{1,0:T(8,128)}), f32[32,512]{1,0:T(8,128)}) %reduce-scatter.15.cloned.1.call-update) | async-done | bytes 65552 | tf_op jit(solution)/shard_map/reduce_scatter | solution.py:304
  882.3 142.9 %reduce-scatter.11.cloned.1.call-done = f32[32,1024]{1,0:T(8,128)} async-done(((f32[1024,1024]{1,0:T(8,128)}), f32[32,1024]{1,0:T(8,128)}) %reduce-scatter.11.cloned.1.call-update) | async-done | bytes 131088 | tf_op jit(solution)/shard_map/reduce_scatter | solution.py:302
  1025.2 143.0 %reduce-scatter.17.cloned.1.call-done = f32[32,1024]{1,0:T(8,128)} async-done(((f32[1024,1024]{1,0:T(8,128)}), f32[32,1024]{1,0:T(8,128)}) %reduce-scatter.17.cloned.1.call-update) | async-done | bytes 131088 | tf_op jit(solution)/shard_map/reduce_scatter | solution.py:305
  (231 shorter events, 83.4 us)
Async XLA Ops:
  7.2 60.3 %all-gather.9.cloned.1.call-start = ((), (), s32[]{:S(2)}) async-start(), calls=%async_computation.12 | async-start | bytes 1081344 | tf_op jit(solution)/shard_map/all_gather | solution.py:147
  7.9 115.3 %all-gather.11.cloned.1.call-start = ((), (), s32[]{:S(2)}) async-start(), calls=%async_computation.13 | async-start | bytes 1081344 | tf_op jit(solution)/shard_map/all_gather | solution.py:146
  8.7 172.9 %all-gather.13.cloned.1.call-start = ((), (), s32[]{:S(2)}) async-start(), calls=%async_computation.14 | async-start | bytes 2162688 | tf_op jit(solution)/shard_map/all_gather | solution.py:145
  9.4 230.3 %all-gather.15.cloned.1.call-start = ((), (), s32[]{:S(2)}) async-start(), calls=%async_computation.15 | async-start | bytes 2162688 | tf_op jit(solution)/shard_map/all_gather | solution.py:148
  10.0 251.3 %all-gather.17.cloned.1.call-start = ((), (), s32[]{:S(2)}) async-start(), calls=%async_computation.16 | async-start | bytes 1572864 | tf_op jit(solution)/shard_map/all_gather | solution.py:153
  10.6 273.4 %all-gather.19.cloned.1.call-start = ((), (), s32[]{:S(2)}) async-start(), calls=%async_computation.17 | async-start | bytes 1572864 | tf_op jit(solution)/shard_map/all_gather | solution.py:154
  11.8 385.4 %copy-start.55 = (f32[128]{0:T(128)}, f32[128]{0:T(128)S(1)}, u32[]{:S(2)}) copy-start(f32[128]{0:T(128)S(1)} %compare_convert_fusion) | copy-start | bytes 1540
  13.5 171.5 %copy-start.50 = (pred[128,128]{0,1:T(8,128)(4,1)}, pred[128,128]{0,1:T(8,128)(4,1)S(1)}, u32[]{:S(2)}) copy-start(pred[128,128]{0,1:T(8,128)(4,1)S(1)} %compare_and_fusion.1) | copy-start | bytes 49156
  58.2 183.6 %copy-start.41 = (f32[1024]{0:T(1024)}, f32[1024]{0:T(1024)S(1)}, u32[]{:S(2)}) copy-start(f32[1024]{0:T(1024)S(1)} %convert_element_type.161) | copy-start | bytes 12292
  59.2 333.1 %copy-start.39 = (f32[16,128]{1,0:T(8,128)}, f32[16,128]{1,0:T(8,128)S(1)}, u32[]{:S(2)}) copy-start(f32[16,128]{1,0:T(8,128)S(1)} %get-tuple-element.42) | copy-start | bytes 24580
  59.2 338.0 %copy-start.33 = (f32[128,16]{0,1:T(8,128)}, f32[128,16]{0,1:T(8,128)S(1)}, u32[]{:S(2)}) copy-start(f32[128,16]{0,1:T(8,128)S(1)} %get-tuple-element.43) | copy-start | bytes 24580
  244.0 23.2 %all-to-all-start = ((bf16[16,24,1024]{2,1,0:T(8,128)(2,1)}), bf16[16,24,1024]{2,1,0:T(8,128)(2,1)S(1)}, u32[]{:S(2)}, u32[]{:S(2)}) async-start(bf16[16,24,1024]{2,1,0:T(8,128)(2,1)} %convolution_convert_fusion.4), calls=%async_computation | async-start | bytes 1572864 | tf_op jit(solution)/shard_map/all_to_all | solution.py:194
  248.5 58.3 %all-gather.21.cloned.1.call-start = ((), (), s32[]{:S(2)}) async-start(), calls=%async_computation.18 | async-start | bytes 1572864 | tf_op jit(solution)/shard_map/all_gather | solution.py:155
  309.6 82.3 %all-to-all-start.1 = ((bf16[16,24,1024]{2,1,0:T(8,128)(2,1)}), bf16[16,24,1024]{2,1,0:T(8,128)(2,1)S(1)}, u32[]{:S(2)}, u32[]{:S(2)}) async-start(bf16[16,24,1024]{2,1,0:T(8,128)(2,1)} %bitcast.18), calls=%async_computation.1 | async-start | bytes 1572864 | tf_op jit(solution)/shard_map/all_to_all | solution.py:197
  393.6 22.3 %all-to-all-start.2 = ((bf16[16,24,1024]{2,1,0:T(8,128)(2,1)}), bf16[16,24,1024]{2,1,0:T(8,128)(2,1)S(1)}, u32[]{:S(2)}, u32[]{:S(2)}) async-start(bf16[16,24,1024]{2,1,0:T(8,128)(2,1)} %multiply_convert_fusion), calls=%async_computation.2 | async-start | bytes 1572864 | tf_op jit(solution)/shard_map/all_to_all | solution.py:237
  397.2 140.4 %reduce-scatter.25.cloned.1.call-start = ((), (), s32[]{:S(2)}) async-start(), calls=%async_computation.26 | async-start | bytes 540672
  399.0 182.6 %reduce-scatter.19.cloned.1.call-start = ((), (), s32[]{:S(2)}) async-start(), calls=%async_computation.23 | async-start | bytes 1572864 | tf_op jit(solution)/shard_map/reduce_scatter | solution.py:310
  421.2 162.6 %reduce-scatter.21.cloned.1.call-start = ((), (), s32[]{:S(2)}) async-start(), calls=%async_computation.24 | async-start | bytes 1572864 | tf_op jit(solution)/shard_map/reduce_scatter | solution.py:313
  426.2 24.5 %all-to-all-start.3 = ((bf16[16,24,1024]{2,1,0:T(8,128)(2,1)}), bf16[16,24,1024]{2,1,0:T(8,128)(2,1)}, u32[]{:S(2)}, u32[]{:S(2)}) async-start(bf16[16,24,1024]{2,1,0:T(8,128)(2,1)} %bitcast.25), calls=%async_computation.3 | async-start | bytes 1572864 | tf_op jit(solution)/shard_map/all_to_all | solution.py:241
  432.0 170.9 %reduce-scatter.23.cloned.1.call-start = ((), (), s32[]{:S(2)}) async-start(), calls=%async_computation.25 | async-start | bytes 1572864 | tf_op jit(solution)/shard_map/reduce_scatter | solution.py:316
  442.1 302.8 %reduce-scatter.13.cloned.1.call-start = ((), (), s32[]{:S(2)}) async-start(), calls=%async_computation.20 | async-start | bytes 2162688 | tf_op jit(solution)/shard_map/reduce_scatter | solution.py:303
  459.5 422.8 %reduce-scatter.15.cloned.1.call-start = ((), (), s32[]{:S(2)}) async-start(), calls=%async_computation.21 | async-start | bytes 2162688 | tf_op jit(solution)/shard_map/reduce_scatter | solution.py:304
  463.5 561.6 %reduce-scatter.11.cloned.1.call-start = ((), (), s32[]{:S(2)}) async-start(), calls=%async_computation.19 | async-start | bytes 4325376 | tf_op jit(solution)/shard_map/reduce_scatter | solution.py:302
  468.6 699.5 %reduce-scatter.17.cloned.1.call-start = ((), (), s32[]{:S(2)}) async-start(), calls=%async_computation.22 | async-start | bytes 4325376 | tf_op jit(solution)/shard_map/reduce_scatter | solution.py:305
  (52 other events, 1247.1 us)
Sparse Core Ops, SparseCore 0:
  10.9 56.5 all-gather.8
  70.4 52.8 all-gather.10
  126.2 55.3 all-gather.12
  184.4 55.1 all-gather.14
  241.1 20.1 all-gather.16
  262.6 21.2 all-gather.18
  285.5 21.2 all-gather.20
  400.3 137.3 reduce-scatter.24
  540.4 17.0 reduce-scatter.18
  559.6 20.5 reduce-scatter.20
  582.4 20.4 reduce-scatter.22
  605.6 139.2 reduce-scatter.12
  747.7 134.5 reduce-scatter.14
  885.0 140.1 reduce-scatter.10
  1027.9 140.2 reduce-scatter.16
where the time goes:
time: 1180 us; the launch traced here: 1170 us
  waiting for transfers between devices  901 us (76%)
  blocking collectives  156 us (13%)
  matrix products  51.4 us (4%)
  starting transfers between devices  20 us (2%)
  other arithmetic  18.5 us (2%)
  between operations  14.8 us (1%)
  local copies, waits for them, and re-layouts  12.5 us (1%)
    reduce_scatter x1, waiting for transfers between devices, shards(): lax.psum_scatter(grad_w_output, ('dp', 'fsdp'), scatter_dimension=0, tile...  143 us
    reduce_scatter x1, waiting for transfers between devices, shards(): lax.psum_scatter(grad_w_query, ('dp', 'fsdp'), scatter_dimension=0, tiled...  143 us
    reduce_scatter x1, waiting for transfers between devices, shards(): lax.psum_scatter(grad_w_key, ('dp', 'fsdp'), scatter_dimension=0, tiled=T...  140 us
    reduce_scatter x1, waiting for transfers between devices, shards(): lax.psum_scatter(grad_w_value, ('dp', 'fsdp'), scatter_dimension=0, tiled...  137 us
    unnamed x2, blocking collectives  80 us
    all_gather x1, blocking collectives, shards(): lax.all_gather(router_weight, ('dp', 'fsdp'), axis=0, tiled=True)  76.2 us
    unnamed x16, waiting for transfers between devices  69.8 us
    all_gather x1, waiting for transfers between devices, shards(): lax.all_gather(query_weight, ('dp', 'fsdp'), axis=0, tiled=True)  56.5 us
  transfers between devices with their start and end apart: 19, of which 16 were waited for; matrix products, arithmetic and copies ran while one was open for 6% of the time, Pallas kernels for 0%

commit v1 on v0

--- a/solution.py
+++ b/solution.py
@@ -1,6 +1,10 @@
+import functools
+
 import jax
 import jax.numpy as jnp
 from jax import lax
+from jax.experimental import pallas as pl
+from jax.experimental.pallas import tpu as pltpu
 from jax.sharding import PartitionSpec as P
 
 HEADS = 16
@@ -121,7 +125,209 @@
     return (grad_rows_in, grad_gate_w, grad_up_w, grad_down_w)
 
 
+def axis_bits(size):
+    return size.bit_length() - 1
+
+
+def is_cube(sizes):
+    return all(size & (size - 1) == 0 for size in sizes) and sizes[0] > 1
+
+
+def span(bits):
+    masks = [0]
+    for bit in bits:
+        masks = masks + [mask | (1 << bit) for mask in masks]
+    return masks
+
+
+def stream_orders(sizes):
+    dp_bits, fsdp_bits = (axis_bits(sizes[0]), axis_bits(sizes[1]))
+    low = [bit for bit in range(fsdp_bits)]
+    high = [fsdp_bits + bit for bit in range(dp_bits - 1, 0, -1)]
+    core = [fsdp_bits]
+    return (high + low + core, high[:-1] + low + high[-1:] + core)
+
+
+class Cube:
+    def __init__(self, sizes):
+        self.sizes = sizes
+        self.dp = lax.axis_index("dp")
+        self.fsdp = lax.axis_index("fsdp")
+        self.me = self.dp * sizes[1] + self.fsdp
+        self.fsdp_bits = axis_bits(sizes[1])
+        self.flips = [
+            (1 - 2 * ((self.me // (1 << bit)) % 2)) * (1 << bit)
+            for bit in range(axis_bits(sizes[0]) + self.fsdp_bits)
+        ]
+
+    def block(self, mask):
+        index = self.me
+        for bit, flip in enumerate(self.flips):
+            if mask >> bit & 1:
+                index = index + flip
+        return index
+
+    def partner(self, bit):
+        other = self.me + self.flips[bit]
+        return {"dp": other // self.sizes[1], "fsdp": other % self.sizes[1]}
+
+    def greet(self):
+        barrier = pltpu.get_barrier_semaphore()
+        for bit in range(len(self.flips)):
+            pl.semaphore_signal(
+                barrier, inc=1, device_id=self.partner(bit), device_id_type=pl.DeviceIdType.MESH
+            )
+        pl.semaphore_wait(barrier, len(self.flips))
+
+
+def gather_kernel(sizes, a_ref, b_ref, a_out, b_out, local_sems, send_sems, recv_sems):
+    cube = Cube(sizes)
+    cube.greet()
+    orders = stream_orders(sizes)
+    streams = ((a_ref, a_out), (b_ref, b_out))
+    copies = ({}, {})
+    arrived = (set(), set())
+    own = []
+    for which, (source, target) in enumerate(streams):
+        own.append(pltpu.make_async_copy(source, target.at[cube.me], local_sems.at[which]))
+        own[-1].start()
+    for stage in range(len(orders[0])):
+        counts = len(span(orders[0][:stage]))
+        for place in range(counts):
+            for which, (source, target) in enumerate(streams):
+                order = orders[which]
+                mask = span(order[:stage])[place]
+                if mask and mask not in arrived[which]:
+                    copies[which][mask].wait_recv()
+                    arrived[which].add(mask)
+                label = mask | (1 << order[stage])
+                copy = pltpu.make_async_remote_copy(
+                    src_ref=target.at[cube.block(mask)] if mask else source,
+                    dst_ref=target.at[cube.block(mask)],
+                    send_sem=send_sems.at[which, label],
+                    recv_sem=recv_sems.at[which, label],
+                    device_id=cube.partner(order[stage]),
+                    device_id_type=pl.DeviceIdType.MESH,
+                )
+                copy.start()
+                copies[which][label] = copy
+    for which in range(2):
+        for label, copy in copies[which].items():
+            if label not in arrived[which]:
+                copy.wait_recv()
+        for copy in copies[which].values():
+            copy.wait_send()
+        own[which].wait()
+
+
+def gather_rows(sizes, packed_a, packed_b):
+    blocks = sizes[0] * sizes[1]
+    if not is_cube(sizes):
+        return tuple(
+            lax.all_gather(packed, ("dp", "fsdp"), axis=0) for packed in (packed_a, packed_b)
+        )
+    return pl.pallas_call(
+        lambda *refs: gather_kernel(sizes, *refs),
+        out_shape=tuple(
+            jax.ShapeDtypeStruct((blocks,) + packed.shape, packed.dtype)
+            for packed in (packed_a, packed_b)
+        ),
+        in_specs=[pl.BlockSpec(memory_space=pl.ANY)] * 2,
+        out_specs=(pl.BlockSpec(memory_space=pl.ANY),) * 2,
+        scratch_shapes=[
+            pltpu.SemaphoreType.DMA((2,)),
+            pltpu.SemaphoreType.DMA((2, blocks)),
+            pltpu.SemaphoreType.DMA((2, blocks)),
+        ],
+        compiler_params=pltpu.CompilerParams(collective_id=0, has_side_effects=True),
+        name="gather_rows",
+    )(packed_a, packed_b)
+
+
+def scatter_kernel(
+    sizes, a_ref, b_ref, a_out, b_out, a_slots, b_slots, a_held, b_held, send_sems, recv_sems
+):
+    cube = Cube(sizes)
+    cube.greet()
+    orders = [order[::-1] for order in stream_orders(sizes)]
+    streams = ((a_ref, a_out, a_slots, a_held), (b_ref, b_out, b_slots, b_held))
+    copies = ({}, {})
+    places = ({}, {})
+
+    def total(which, mask, stage):
+        source, _, slots, _ = streams[which]
+        value = source[cube.block(mask)].astype(jnp.float32)
+        for earlier in orders[which][:stage]:
+            label = mask | (1 << earlier)
+            copies[which][label].wait_recv()
+            value = value + slots[label].astype(jnp.float32)
+        return value
+
+    for stage in range(len(orders[0])):
+        for place in range(len(span(orders[0][stage + 1 :]))):
+            for which, (source, _, slots, held) in enumerate(streams):
+                order = orders[which]
+                masks = span(order[stage + 1 :][::-1])
+                masks.sort(
+                    key=lambda mask: [
+                        at for at, bit in enumerate(order) if mask >> bit & 1
+                    ][:1]
+                    or [len(order)]
+                )
+                mask = masks[place] | (1 << order[stage])
+                if stage == 0:
+                    leaving = source.at[cube.block(mask)]
+                else:
+                    slot = places[which].setdefault(mask, len(places[which]))
+                    held[slot] = total(which, mask, stage).astype(jnp.bfloat16)
+                    leaving = held.at[slot]
+                copy = pltpu.make_async_remote_copy(
+                    src_ref=leaving,
+                    dst_ref=slots.at[mask],
+                    send_sem=send_sems.at[which, mask],
+                    recv_sem=recv_sems.at[which, mask],
+                    device_id=cube.partner(order[stage]),
+                    device_id_type=pl.DeviceIdType.MESH,
+                )
+                copy.start()
+                copies[which][mask] = copy
+    for which, (_, out, _, _) in enumerate(streams):
+        out[...] = total(which, 0, len(orders[which]))
+    for which in range(2):
+        for copy in copies[which].values():
+            copy.wait_send()
+
+
+def scatter_rows(sizes, packed_a, packed_b):
+    blocks = sizes[0] * sizes[1]
+    if not is_cube(sizes):
+        return tuple(
+            lax.psum_scatter(packed.astype(jnp.float32), ("dp", "fsdp"), scatter_dimension=0)
+            for packed in (packed_a, packed_b)
+        )
+    shapes = [packed.shape[1:] for packed in (packed_a, packed_b)]
+    return pl.pallas_call(
+        lambda *refs: scatter_kernel(sizes, *refs),
+        out_shape=tuple(jax.ShapeDtypeStruct(shape, jnp.float32) for shape in shapes),
+        in_specs=[pl.BlockSpec(memory_space=pltpu.VMEM)] * 2,
+        out_specs=(pl.BlockSpec(memory_space=pltpu.VMEM),) * 2,
+        scratch_shapes=[
+            pltpu.VMEM((blocks,) + shapes[0], jnp.bfloat16),
+            pltpu.VMEM((blocks,) + shapes[1], jnp.bfloat16),
+            pltpu.VMEM((blocks // 2,) + shapes[0], jnp.bfloat16),
+            pltpu.VMEM((blocks // 2,) + shapes[1], jnp.bfloat16),
+            pltpu.SemaphoreType.DMA((2, blocks)),
+            pltpu.SemaphoreType.DMA((2, blocks)),
+        ],
+        compiler_params=pltpu.CompilerParams(
+            collective_id=1, has_side_effects=True, vmem_limit_bytes=48 * 1024 * 1024
+        ),
+        name="scatter_rows",
+    )(packed_a, packed_b)
+
+
 def shards(
+    sizes,
     hidden_in,
     doc_id,
     expert_ids,
@@ -140,21 +346,30 @@
     rows = hidden_in.shape[0]
     groups = HEADS // KV_HEADS
     scale = HEAD_DIM ** (-0.5)
-    dense_full = (
-        lax.all_gather(attn_gain, ("dp", "fsdp"), axis=0, tiled=True),
-        lax.all_gather(query_weight, ("dp", "fsdp"), axis=0, tiled=True),
-        lax.all_gather(key_weight, ("dp", "fsdp"), axis=0, tiled=True),
-        lax.all_gather(value_weight, ("dp", "fsdp"), axis=0, tiled=True),
-        lax.all_gather(output_weight, ("dp", "fsdp"), axis=0, tiled=True),
-        lax.all_gather(ffn_gain, ("dp", "fsdp"), axis=0, tiled=True),
-        lax.all_gather(router_weight, ("dp", "fsdp"), axis=0, tiled=True),
-    )
+    experts_all = router_weight.shape[1]
+    query_width, key_width = (query_weight.shape[1], key_weight.shape[1])
+    small_width = -(-(experts_all + 2) // 128) * 128
+    small = jnp.concatenate([router_weight, attn_gain[:, None], ffn_gain[:, None]], axis=1)
+    small = jnp.pad(small, ((0, 0), (0, small_width - small.shape[1])))
+    full_a, full_b = gather_rows(
+        sizes,
+        jnp.concatenate([query_weight, key_weight, small], axis=1),
+        jnp.concatenate([value_weight, output_weight], axis=1),
+    )
+    full_a = full_a.reshape(-1, full_a.shape[2])
+    full_b = full_b.reshape(-1, full_b.shape[2])
+    w_query = full_a[:, :query_width]
+    w_key = full_a[:, query_width : query_width + key_width]
+    full_small = full_a[:, query_width + key_width :]
+    w_router = full_small[:, :experts_all]
+    gain_one, gain_two = (full_small[:, experts_all], full_small[:, experts_all + 1])
+    w_value = full_b[:, : value_weight.shape[1]]
+    w_output = full_b[:, value_weight.shape[1] :]
     expert_full = (
         lax.all_gather(expert_gate, "fsdp", axis=1, tiled=True),
         lax.all_gather(expert_up, "fsdp", axis=1, tiled=True),
         lax.all_gather(expert_down, "fsdp", axis=1, tiled=True),
     )
-    gain_one, w_query, w_key, w_value, w_output, gain_two, w_router = dense_full
     w_gate, w_up, w_down = (expert_full[0][0], expert_full[1][0], expert_full[2][0])
     position, allowed, live_rows = positions_mask(doc_id)
     cosine, sinusoid = rope_tables(position)
@@ -208,22 +423,6 @@
     picked_rows = jnp.take(back_flat, slot_index.reshape(-1), axis=0).reshape(rows, TOP, width)
     expert_sum = jnp.sum(gate_pick[:, :, None] * picked_rows.astype(jnp.float32), axis=1)
     layer_out = (resid_mid + expert_sum).astype(jnp.bfloat16)
-    dense_full = (
-        lax.all_gather(attn_gain, ("dp", "fsdp"), axis=0, tiled=True),
-        lax.all_gather(query_weight, ("dp", "fsdp"), axis=0, tiled=True),
-        lax.all_gather(key_weight, ("dp", "fsdp"), axis=0, tiled=True),
-        lax.all_gather(value_weight, ("dp", "fsdp"), axis=0, tiled=True),
-        lax.all_gather(output_weight, ("dp", "fsdp"), axis=0, tiled=True),
-        lax.all_gather(ffn_gain, ("dp", "fsdp"), axis=0, tiled=True),
-        lax.all_gather(router_weight, ("dp", "fsdp"), axis=0, tiled=True),
-    )
-    expert_full = (
-        lax.all_gather(expert_gate, "fsdp", axis=1, tiled=True),
-        lax.all_gather(expert_up, "fsdp", axis=1, tiled=True),
-        lax.all_gather(expert_down, "fsdp", axis=1, tiled=True),
-    )
-    gain_one, w_query, w_key, w_value, w_output, gain_two, w_router = dense_full
-    w_gate, w_up, w_down = (expert_full[0][0], expert_full[1][0], expert_full[2][0])
     grad_out = out_grad.astype(jnp.float32)
     slot_gate = jnp.sum(dispatch * gates.T[:, None, :], axis=2)
     pulled_grad = jnp.einsum(
@@ -297,14 +496,34 @@
         grad_normed, normed_one, scale_one, gain_one.astype(jnp.float32)
     )
     grad_input = (grad_mid + grad_norm_one).astype(jnp.bfloat16)
+    grad_small = jnp.concatenate(
+        [grad_w_router, grad_gain_one[:, None], grad_gain_two[:, None]], axis=1
+    )
+    grad_small = jnp.pad(grad_small, ((0, 0), (0, small_width - grad_small.shape[1])))
+    blocks = sizes[0] * sizes[1]
+    own_a, own_b = scatter_rows(
+        sizes,
+        jnp.concatenate(
+            [
+                grad_w_query.astype(jnp.bfloat16),
+                grad_w_key.astype(jnp.bfloat16),
+                grad_small.astype(jnp.bfloat16),
+            ],
+            axis=1,
+        ).reshape(blocks, -1, full_a.shape[1]),
+        jnp.concatenate(
+            [grad_w_value.astype(jnp.bfloat16), grad_w_output.astype(jnp.bfloat16)], axis=1
+        ).reshape(blocks, -1, full_b.shape[1]),
+    )
+    own_small = own_a[:, query_width + key_width :]
     dense_grads = (
-        lax.psum_scatter(grad_gain_one, ("dp", "fsdp"), scatter_dimension=0, tiled=True),
-        lax.psum_scatter(grad_w_query, ("dp", "fsdp"), scatter_dimension=0, tiled=True),
-        lax.psum_scatter(grad_w_key, ("dp", "fsdp"), scatter_dimension=0, tiled=True),
-        lax.psum_scatter(grad_w_value, ("dp", "fsdp"), scatter_dimension=0, tiled=True),
-        lax.psum_scatter(grad_w_output, ("dp", "fsdp"), scatter_dimension=0, tiled=True),
-        lax.psum_scatter(grad_gain_two, ("dp", "fsdp"), scatter_dimension=0, tiled=True),
-        lax.psum_scatter(grad_w_router, ("dp", "fsdp"), scatter_dimension=0, tiled=True),
+        own_small[:, experts_all],
+        own_a[:, :query_width],
+        own_a[:, query_width : query_width + key_width],
+        own_b[:, : value_weight.shape[1]],
+        own_b[:, value_weight.shape[1] :],
+        own_small[:, experts_all + 1],
+        own_small[:, :experts_all],
     )
     expert_grads = (
         lax.psum_scatter(
@@ -364,4 +583,6 @@
         P("dp", "fsdp", None),
         P("dp", "fsdp", None),
     )
-    return jax.shard_map(shards, mesh=mesh, in_specs=in_specs, out_specs=out_specs, check_vma=False)
+    sizes = (mesh.shape["dp"], mesh.shape["fsdp"])
+    body = functools.partial(shards, sizes)
+    return jax.shard_map(body, mesh=mesh, in_specs=in_specs, out_specs=out_specs, check_vma=False)

time: 1180 us -> 306 us (0.26)
  waiting for transfers between devices: 901 us -> 42.4 us
  blocking collectives: 156 us -> 25.3 us
  Pallas kernels: 0 us -> 105 us
    reduce_scatter x4 -> x0, waiting for transfers between devices: 563 us -> none  [the longest x1 143 us: shards(): lax.psum_scatter(grad_w_output, ('dp', 'fsdp'), scatter_dimension=0, tile...]
    all_gather x4 -> x0, waiting for transfers between devices: 173 us -> none  [the longest x1 56.5 us: shards(): lax.all_gather(query_weight, ('dp', 'fsdp'), axis=0, tiled=True)]
    pallas_call x0 -> x2, Pallas kernels: none -> 105 us  [the longest x1 58 us: gather_rows(): pl.pallas_call(lambda *refs: gather_kernel(sizes, *refs), out_shape=tuple...]
    unnamed x2 -> x0, blocking collectives: 80 us -> none
    all_gather x1 -> x0, blocking collectives: 76.2 us -> none  [shards(): lax.all_gather(router_weight, ('dp', 'fsdp'), axis=0, tiled=True)]
    unnamed x16 -> x6, waiting for transfers between devices: 69.8 us -> 2.11 us
    all_to_all x0 -> x1, blocking collectives: none -> 25.3 us  [shards(): lax.all_to_all(grad_send, 'dp', split_axis=0, concat_axis=0, tiled=True)]
    all_gather x1, waiting for transfers between devices: 20.2 us -> 0.01 us  [shards(): lax.all_gather(expert_down, 'fsdp', axis=1, tiled=True)]
  transfers between devices with their start and end apart: 19 -> 9, of which waited for: 16 -> 3; matrix products, arithmetic and copies ran while one was open for 6% -> 30% of each run, Pallas kernels for 0% -> 34%
where the time goes in v1:
time: 306 us; the launch traced here: 304 us
  Pallas kernels  105 us (34%)
  matrix products  53.6 us (18%)
  waiting for transfers between devices  42.4 us (14%)
  other arithmetic  26.4 us (9%)
  blocking collectives  25.3 us (8%)
  local copies, waits for them, and re-layouts  21.6 us (7%)
  starting transfers between devices  15.3 us (5%)
  between operations  15 us (5%)
    pallas_call x1, Pallas kernels, gather_rows(): pl.pallas_call(lambda *refs: gather_kernel(sizes, *refs), out_shape=tuple...  58 us
    pallas_call x1, Pallas kernels, scatter_rows(): pl.pallas_call(lambda *refs: scatter_kernel(sizes, *refs), out_shape=tupl...  46.8 us
    all_to_all x1, blocking collectives, shards(): lax.all_to_all(grad_send, 'dp', split_axis=0, concat_axis=0, tiled=True)  25.3 us
    all_to_all x1, waiting for transfers between devices, shards(): lax.all_to_all(send_rows, 'dp', split_axis=0, concat_axis=0, tiled=True)  17.9 us
    all_to_all x1, waiting for transfers between devices, shards(): lax.all_to_all(out_rows.reshape(recv_rows.shape), 'dp', split_axis=0, con...  17.4 us
    convert_element_type x3, other arithmetic, shards(): expert_grads = (lax.psum_scatter(grad_gate_w[None].astype(jnp.bfloat16),...  6.42 us
  transfers between devices with their start and end apart: 9, of which 3 were waited for; matrix products, arithmetic and copies ran while one was open for 30% of the time, Pallas kernels for 34%

profile of v1, /device:TPU:0, one launch (start us, length us, event | category | flops | bytes accessed | tf_op | source)
XLA Modules:
  0.0 304.5 jit_solution(4583631271340262861)
XLA Ops:
  15.5 58.0 %gather_rows.1 = (bf16[32,32,1664]{2,1,0:T(8,128)(2,1)}, bf16[32,32,1536]{2,1,0:T(8,128)(2,1)}) custom-call(bf16[32,1664]{1,0:T(8,128)(2,1)} %pad_maximum_fusion.7.refs_0_, bf16[32,1536]{1,0:T(8,128)(2,1)} %pad_maximum_fusion.8.refs_1_), custom_call_target="tpu_custom_call" | custom-call | tf_op jit(solution)/shard_map/gather_rows/pallas_call | solution.py:229
  75.1 2.6 fusion.8
  83.1 2.2 multiply_reduce_fusion.5
  87.1 5.2 %all-to-all-start = ((bf16[16,24,1024]{2,1,0:T(8,128)(2,1)}), bf16[16,24,1024]{2,1,0:T(8,128)(2,1)S(1)}, u32[]{:S(2)}, u32[]{:S(2)}) async-start(bf16[16,24,1024]{2,1,0:T(8,128)(2,1)} %convolution_convert_fusion.8), calls=%async_computation | async-start | bytes 1572864 | tf_op jit(solution)/shard_map/all_to_all | solution.py:409
  93.0 17.9 %all-to-all-done = bf16[16,24,1024]{2,1,0:T(8,128)(2,1)S(1)} async-done(((bf16[16,24,1024]{2,1,0:T(8,128)(2,1)}), bf16[16,24,1024]{2,1,0:T(8,128)(2,1)S(1)}, u32[]{:S(2)}, u32[]{:S(2)}) %all-to-all-start) | async-done | bytes 786464 | tf_op jit(solution)/shard_map/all_to_all | solution.py:409
  113.7 2.7 multiply_convert_fusion.3
  116.3 2.9 convolution_convert_fusion.7
  119.2 5.4 %all-to-all-start.1 = ((bf16[16,24,1024]{2,1,0:T(8,128)(2,1)}), bf16[16,24,1024]{2,1,0:T(8,128)(2,1)S(1)}, u32[]{:S(2)}, u32[]{:S(2)}) async-start(bf16[16,24,1024]{2,1,0:T(8,128)(2,1)} %bitcast.23), calls=%async_computation.1 | async-start | bytes 1572864 | tf_op jit(solution)/shard_map/all_to_all | solution.py:412
  125.9 17.4 %all-to-all-done.1 = bf16[16,24,1024]{2,1,0:T(8,128)(2,1)S(1)} async-done(((bf16[16,24,1024]{2,1,0:T(8,128)(2,1)}), bf16[16,24,1024]{2,1,0:T(8,128)(2,1)S(1)}, u32[]{:S(2)}, u32[]{:S(2)}) %all-to-all-start.1) | async-done | bytes 786464 | tf_op jit(solution)/shard_map/all_to_all | solution.py:412
  144.2 25.3 %all_to_all.20 = bf16[16,24,1024]{2,1,0:T(8,128)(2,1)S(1)} all-to-all(bf16[16,24,1024]{2,1,0:T(8,128)(2,1)S(1)} %multiply_convert_fusion), channel_id=1, replica_groups=mesh['dp'=16,'fsdp'=2] {'dp'}, dimensions={0} | all-to-all | bytes 1572864 | tf_op jit(solution)/shard_map/all_to_all | solution.py:436
  172.9 2.9 fusion.19
  176.5 2.8 fusion.11
  182.5 4.3 %all-to-all-start.3 = ((bf16[16,24,1024]{2,1,0:T(8,128)(2,1)}), bf16[16,24,1024]{2,1,0:T(8,128)(2,1)}, u32[]{:S(2)}, u32[]{:S(2)}) async-start(bf16[16,24,1024]{2,1,0:T(8,128)(2,1)} %bitcast.30), calls=%async_computation.3 | async-start | bytes 1572864 | tf_op jit(solution)/shard_map/all_to_all | solution.py:440
  189.4 4.5 %gather_fusion = bf16[1024,1024]{1,0:T(8,128)(2,1)S(1)} fusion(bf16[384,1024]{1,0:T(8,128)(2,1)S(1)} %bitcast.134, s32[1024]{0:T(1024)} %broadcast_clamp_fusion), kind=kCustom, calls=%fused_computation | custom fusion | bytes 4198400 | tf_op jit(solution)/shard_map/jit(_take)/gather | solution.py:423
  195.5 3.2 %multiply_reduce_fusion = f32[128,1024]{1,0:T(8,128)} fusion(bf16[1024,1024]{1,0:T(8,128)(2,1)S(1)} %gather_fusion, f32[128,8]{1,0:T(8,128)} %copy.77, pred[128,8]{1,0:T(8,128)(4,1)} %copy.78), kind=kLoop, calls=%fused_computation.3 | loop fusion | flops 4063232 | bytes 2626560 | tf_op jit(solution)/shard_map/reduce_sum | solution.py:424
  200.6 4.9 %all-to-all-done.3 = bf16[16,24,1024]{2,1,0:T(8,128)(2,1)} async-done(((bf16[16,24,1024]{2,1,0:T(8,128)(2,1)}), bf16[16,24,1024]{2,1,0:T(8,128)(2,1)}, u32[]{:S(2)}, u32[]{:S(2)}) %all-to-all-start.3) | async-done | bytes 786464 | tf_op jit(solution)/shard_map/all_to_all | solution.py:440
  216.9 2.4 fusion.6
  221.7 2.7 fusion.59
  225.7 3.6 %copy.84 = bf16[1024,1664]{1,0:T(8,128)(2,1)} copy(bf16[1024,1664]{0,1:T(8,128)(2,1)S(1)} %pad_maximum_fusion) | data formatting | bytes 6815744 | tf_op jit(solution)/shard_map/concatenate | solution.py:506
  234.8 3.4 %copy.85 = bf16[1024,1536]{1,0:T(8,128)(2,1)S(1)} copy(bf16[1024,1536]{0,1:T(8,128)(2,1)} %pad_maximum_fusion.1) | data formatting | bytes 6291456 | tf_op jit(solution)/shard_map/concatenate | solution.py:514
  238.2 46.8 %scatter_rows.1 = (f32[32,1664]{1,0:T(8,128)S(1)}, f32[32,1536]{1,0:T(8,128)S(1)}) custom-call(bf16[32,32,1664]{2,1,0:T(8,128)(2,1)} %bitcast.135, bf16[32,32,1536]{2,1,0:T(8,128)(2,1)S(1)} %bitcast.133), custom_call_target="tpu_custom_call" | custom-call | tf_op jit(solution)/shard_map/scatter_rows/pallas_call | solution.py:309
  289.0 2.2 fusion.58
  291.2 2.1 convert_element_type.225
  293.4 2.1 convert_element_type.228
  (206 shorter events, 61.7 us)
Async XLA Ops:
  7.2 67.8 %copy-start = (bf16[128,1024]{1,0:T(8,128)(2,1)S(1)}, bf16[128,1024]{1,0:T(8,128)(2,1)}, u32[]{:S(2)}) copy-start(bf16[128,1024]{1,0:T(8,128)(2,1)} %param.14) | copy-start | bytes 786436
  7.2 85.8 %all-gather.4.cloned.1.call-start = ((), (), s32[]{:S(2)}) async-start(), calls=%async_computation.7 | async-start | bytes 1572864 | tf_op jit(solution)/shard_map/all_gather | solution.py:369
  7.9 104.9 %all-gather.6.cloned.1.call-start = ((), (), s32[]{:S(2)}) async-start(), calls=%async_computation.8 | async-start | bytes 1572864 | tf_op jit(solution)/shard_map/all_gather | solution.py:370
  9.3 166.5 %copy-start.48 = (f32[128]{0:T(128)}, f32[128]{0:T(128)S(1)}, u32[]{:S(2)}) copy-start(f32[128]{0:T(128)S(1)} %compare_convert_fusion) | copy-start | bytes 1540
  79.6 93.3 %copy-start.42 = (pred[128,128]{0,1:T(8,128)(4,1)}, pred[128,128]{0,1:T(8,128)(4,1)S(1)}, u32[]{:S(2)}) copy-start(pred[128,128]{0,1:T(8,128)(4,1)S(1)} %compare_and_fusion.1) | copy-start | bytes 49156
  85.3 27.4 %copy-start.2 = (f32[128,1024]{1,0:T(8,128)}, f32[128,1024]{1,0:T(8,128)S(1)}, u32[]{:S(2)}) copy-start(f32[128,1024]{1,0:T(8,128)S(1)} %get-tuple-element.89) | copy-start | bytes 1572868
  85.3 27.4 %copy-start.46 = (f32[128]{0:T(128)}, f32[128]{0:T(128)S(1)}, u32[]{:S(2)}) copy-start(f32[128]{0:T(128)S(1)} %add_rsqrt_fusion) | copy-start | bytes 1540
  85.5 27.2 %copy-start.38 = (f32[1024,1]{0,1:T(1,128)}, f32[1024,1]{0,1:T(1,128)S(1)}, u32[]{:S(2)}) copy-start(f32[1024,1]{0,1:T(1,128)S(1)} %copy.101) | copy-start | bytes 12292
  85.7 58.1 %copy-start.36 = (f32[16,128]{1,0:T(8,128)}, f32[16,128]{1,0:T(8,128)S(1)}, u32[]{:S(2)}) copy-start(f32[16,128]{1,0:T(8,128)S(1)} %get-tuple-element.86) | copy-start | bytes 24580
  85.7 101.4 %copy-start.26 = (f32[128,16]{0,1:T(8,128)}, f32[128,16]{0,1:T(8,128)S(1)}, u32[]{:S(2)}) copy-start(f32[128,16]{0,1:T(8,128)S(1)} %get-tuple-element.87) | copy-start | bytes 24580
  87.1 23.9 %all-to-all-start = ((bf16[16,24,1024]{2,1,0:T(8,128)(2,1)}), bf16[16,24,1024]{2,1,0:T(8,128)(2,1)S(1)}, u32[]{:S(2)}, u32[]{:S(2)}) async-start(bf16[16,24,1024]{2,1,0:T(8,128)(2,1)} %convolution_convert_fusion.8), calls=%async_computation | async-start | bytes 1572864 | tf_op jit(solution)/shard_map/all_to_all | solution.py:409
  92.3 24.1 %all-gather.8.cloned.1.call-start = ((), (), s32[]{:S(2)}) async-start(), calls=%async_computation.9 | async-start | bytes 1572864 | tf_op jit(solution)/shard_map/all_gather | solution.py:371
  116.3 27.4 %copy-start.24 = (bf16[384,512]{1,0:T(8,128)(2,1)}, bf16[384,512]{1,0:T(8,128)(2,1)S(1)}, u32[]{:S(2)}) copy-start(bf16[384,512]{1,0:T(8,128)(2,1)S(1)} %get-tuple-element.90) | copy-start | bytes 1179652
  116.3 27.0 %copy-start.11 = (bf16[128,1024]{1,0:T(8,128)(2,1)S(1)}, bf16[128,1024]{1,0:T(8,128)(2,1)}, u32[]{:S(2)}) copy-start(bf16[128,1024]{1,0:T(8,128)(2,1)} %param.17) | copy-start | bytes 786436
  119.2 24.1 %all-to-all-start.1 = ((bf16[16,24,1024]{2,1,0:T(8,128)(2,1)}), bf16[16,24,1024]{2,1,0:T(8,128)(2,1)S(1)}, u32[]{:S(2)}, u32[]{:S(2)}) async-start(bf16[16,24,1024]{2,1,0:T(8,128)(2,1)} %bitcast.23), calls=%async_computation.1 | async-start | bytes 1572864 | tf_op jit(solution)/shard_map/all_to_all | solution.py:412
  124.6 166.6 %reduce-scatter.4.cloned.1.call-start = ((), (), s32[]{:S(2)}) async-start(), calls=%async_computation.10 | async-start | bytes 1572864 | tf_op jit(solution)/shard_map/reduce_scatter | solution.py:529
  143.3 26.1 %copy-start.17 = (f32[384,512]{1,0:T(8,128)S(1)}, f32[384,512]{1,0:T(8,128)}, u32[]{:S(2)}) copy-start(f32[384,512]{1,0:T(8,128)} %copy-done.16) | copy-start | bytes 2359300
  143.3 26.1 %copy-start.51 = (bf16[1,512,1024]{2,1,0:T(8,128)(2,1)S(1)}, bf16[1,512,1024]{2,1,0:T(8,128)(2,1)}, u32[]{:S(2)}) copy-start(bf16[1,512,1024]{2,1,0:T(8,128)(2,1)} %all-gather.8.cloned.1.call-done) | copy-start | bytes 3145732
  143.3 26.1 %copy-start.52 = (f32[384,512]{1,0:T(8,128)S(1)}, f32[384,512]{1,0:T(8,128)}, u32[]{:S(2)}) copy-start(f32[384,512]{1,0:T(8,128)} %get-tuple-element.91) | copy-start | bytes 2359300
  172.9 120.5 %reduce-scatter.6.cloned.1.call-start = ((), (), s32[]{:S(2)}) async-start(), calls=%async_computation.11 | async-start | bytes 1572864 | tf_op jit(solution)/shard_map/reduce_scatter | solution.py:532
  182.5 23.0 %all-to-all-start.3 = ((bf16[16,24,1024]{2,1,0:T(8,128)(2,1)}), bf16[16,24,1024]{2,1,0:T(8,128)(2,1)}, u32[]{:S(2)}, u32[]{:S(2)}) async-start(bf16[16,24,1024]{2,1,0:T(8,128)(2,1)} %bitcast.30), calls=%async_computation.3 | async-start | bytes 1572864 | tf_op jit(solution)/shard_map/all_to_all | solution.py:440
  186.8 108.7 %reduce-scatter.8.cloned.1.call-start = ((), (), s32[]{:S(2)}) async-start(), calls=%async_computation.12 | async-start | bytes 1572864 | tf_op jit(solution)/shard_map/reduce_scatter | solution.py:535
  195.5 11.7 %copy-start.40 = (bf16[128,16]{0,1:T(8,128)(2,1)S(1)}, bf16[128,16]{0,1:T(8,128)(2,1)}, u32[]{:S(2)}) copy-start(bf16[128,16]{0,1:T(8,128)(2,1)} %get-tuple-element.82) | copy-start | bytes 12292
  195.5 11.7 %copy-start.47 = (f32[128]{0:T(128)S(1)}, f32[128]{0:T(128)}, u32[]{:S(2)}) copy-start(f32[128]{0:T(128)} %copy-done.46) | copy-start | bytes 1540
  (38 other events, 169.5 us)
Sparse Core Ops, SparseCore 0:
  9.5 24.5 all-gather.3
  35.7 35.7 all-gather.5
  94.6 21.6 all-gather.7
  173.0 18.7 reduce-scatter.3
  193.8 20.3 reduce-scatter.5
  216.4 20.3 reduce-scatter.7

commit v2 on v1

--- a/solution.py
+++ b/solution.py
@@ -145,7 +145,10 @@
     low = [bit for bit in range(fsdp_bits)]
     high = [fsdp_bits + bit for bit in range(dp_bits - 1, 0, -1)]
     core = [fsdp_bits]
-    return (high + low + core, high[:-1] + low + high[-1:] + core)
+    return (
+        high[:-1] + low + high[-1:] + core,
+        high[:-2] + low + high[-1:] + high[-2:-1] + core,
+    )
 
 
 class Cube:
@@ -191,15 +194,17 @@
     for which, (source, target) in enumerate(streams):
         own.append(pltpu.make_async_copy(source, target.at[cube.me], local_sems.at[which]))
         own[-1].start()
-    for stage in range(len(orders[0])):
-        counts = len(span(orders[0][:stage]))
-        for place in range(counts):
-            for which, (source, target) in enumerate(streams):
-                order = orders[which]
-                mask = span(order[:stage])[place]
-                if mask and mask not in arrived[which]:
-                    copies[which][mask].wait_recv()
-                    arrived[which].add(mask)
+    stages = len(orders[0])
+    places = sorted(range(1 << stages), key=lambda place: (place.bit_count(), place))
+    for place in places:
+        for which, (source, target) in enumerate(streams):
+            order = orders[which]
+            mask = span(order)[place]
+            later = range(place.bit_length(), stages)
+            if mask and len(later):
+                copies[which][mask].wait_recv()
+                arrived[which].add(mask)
+            for stage in later:
                 label = mask | (1 << order[stage])
                 copy = pltpu.make_async_remote_copy(
                     src_ref=target.at[cube.block(mask)] if mask else source,
@@ -244,15 +249,15 @@
     )(packed_a, packed_b)
 
 
-def scatter_kernel(
-    sizes, a_ref, b_ref, a_out, b_out, a_slots, b_slots, a_held, b_held, send_sems, recv_sems
-):
+def scatter_kernel(sizes, width, *refs):
     cube = Cube(sizes)
     cube.greet()
-    orders = [order[::-1] for order in stream_orders(sizes)]
-    streams = ((a_ref, a_out, a_slots, a_held), (b_ref, b_out, b_slots, b_held))
-    copies = ({}, {})
-    places = ({}, {})
+    two_orders = [order[::-1] for order in stream_orders(sizes)]
+    orders = [two_orders[which % 2] for which in range(width)]
+    streams = [refs[which : 4 * width : width] for which in range(width)]
+    send_sems, recv_sems = refs[4 * width :]
+    copies = [{} for _ in range(width)]
+    places = [{} for _ in range(width)]
 
     def total(which, mask, stage):
         source, _, slots, _ = streams[which]
@@ -293,37 +298,34 @@
                 copies[which][mask] = copy
     for which, (_, out, _, _) in enumerate(streams):
         out[...] = total(which, 0, len(orders[which]))
-    for which in range(2):
+    for which in range(width):
         for copy in copies[which].values():
             copy.wait_send()
 
 
-def scatter_rows(sizes, packed_a, packed_b):
+def scatter_rows(sizes, *grads):
     blocks = sizes[0] * sizes[1]
+    packed = [grad.reshape((blocks, -1) + grad.shape[1:]) for grad in grads]
     if not is_cube(sizes):
         return tuple(
-            lax.psum_scatter(packed.astype(jnp.float32), ("dp", "fsdp"), scatter_dimension=0)
-            for packed in (packed_a, packed_b)
+            lax.psum_scatter(part.astype(jnp.float32), ("dp", "fsdp"), scatter_dimension=0)
+            for part in packed
         )
-    shapes = [packed.shape[1:] for packed in (packed_a, packed_b)]
+    width = len(packed)
+    shapes = [part.shape[1:] for part in packed]
     return pl.pallas_call(
-        lambda *refs: scatter_kernel(sizes, *refs),
+        lambda *refs: scatter_kernel(sizes, width, *refs),
         out_shape=tuple(jax.ShapeDtypeStruct(shape, jnp.float32) for shape in shapes),
-        in_specs=[pl.BlockSpec(memory_space=pltpu.VMEM)] * 2,
-        out_specs=(pl.BlockSpec(memory_space=pltpu.VMEM),) * 2,
-        scratch_shapes=[
-            pltpu.VMEM((blocks,) + shapes[0], jnp.bfloat16),
-            pltpu.VMEM((blocks,) + shapes[1], jnp.bfloat16),
-            pltpu.VMEM((blocks // 2,) + shapes[0], jnp.bfloat16),
-            pltpu.VMEM((blocks // 2,) + shapes[1], jnp.bfloat16),
-            pltpu.SemaphoreType.DMA((2, blocks)),
-            pltpu.SemaphoreType.DMA((2, blocks)),
-        ],
+        in_specs=[pl.BlockSpec(memory_space=pltpu.VMEM)] * width,
+        out_specs=(pl.BlockSpec(memory_space=pltpu.VMEM),) * width,
+        scratch_shapes=[pltpu.VMEM((blocks,) + shape, jnp.bfloat16) for shape in shapes]
+        + [pltpu.VMEM((blocks // 2,) + shape, jnp.bfloat16) for shape in shapes]
+        + [pltpu.SemaphoreType.DMA((width, blocks))] * 2,
         compiler_params=pltpu.CompilerParams(
             collective_id=1, has_side_effects=True, vmem_limit_bytes=48 * 1024 * 1024
         ),
         name="scatter_rows",
-    )(packed_a, packed_b)
+    )(*packed)
 
 
 def shards(
@@ -406,7 +408,19 @@
     send_rows = jnp.einsum(
         "ecr,rd->ecd", dispatch_b, routed_in, preferred_element_type=jnp.float32
     ).astype(jnp.bfloat16)
-    recv_rows = lax.all_to_all(send_rows, "dp", split_axis=0, concat_axis=0, tiled=True)
+    slot_gate = jnp.sum(dispatch * gates.T[:, None, :], axis=2)
+    pulled_grad = jnp.einsum(
+        "ecr,rd->ecd", dispatch_b, out_grad, preferred_element_type=jnp.float32
+    )
+    grad_send = (slot_gate[:, :, None] * pulled_grad).astype(jnp.bfloat16)
+    recv_both = lax.all_to_all(
+        jnp.concatenate([send_rows, grad_send], axis=1),
+        "dp",
+        split_axis=0,
+        concat_axis=0,
+        tiled=True,
+    )
+    recv_rows, grad_recv = jnp.split(recv_both, 2, axis=1)
     flat_in = recv_rows.reshape(-1, recv_rows.shape[2])
     gate_pre, up_pre, act_rows, out_rows = expert_forward(flat_in, w_gate, w_up, w_down)
     back_rows = lax.all_to_all(
@@ -424,16 +438,10 @@
     expert_sum = jnp.sum(gate_pick[:, :, None] * picked_rows.astype(jnp.float32), axis=1)
     layer_out = (resid_mid + expert_sum).astype(jnp.bfloat16)
     grad_out = out_grad.astype(jnp.float32)
-    slot_gate = jnp.sum(dispatch * gates.T[:, None, :], axis=2)
-    pulled_grad = jnp.einsum(
-        "ecr,rd->ecd", dispatch_b, out_grad, preferred_element_type=jnp.float32
-    )
-    grad_send = (slot_gate[:, :, None] * pulled_grad).astype(jnp.bfloat16)
     slot_dot = jnp.sum(back_rows.astype(jnp.float32) * pulled_grad, axis=2)
     grad_gates = jnp.sum(dispatch * slot_dot[:, :, None], axis=1).T
     grad_logits = gates * (grad_gates - jnp.sum(gates * grad_gates, axis=1, keepdims=True))
     grad_logits_b = grad_logits.astype(jnp.bfloat16)
-    grad_recv = lax.all_to_all(grad_send, "dp", split_axis=0, concat_axis=0, tiled=True)
     grad_rows_in, grad_gate_w, grad_up_w, grad_down_w = expert_backward(
         flat_in, gate_pre, up_pre, act_rows, grad_recv.reshape(flat_in.shape), w_gate, w_up, w_down
     )
@@ -486,8 +494,11 @@
         .astype(jnp.bfloat16)
     )
     grad_value_b = grad_value_raw.reshape(rows, KV_HEADS * HEAD_DIM).astype(jnp.bfloat16)
-    grad_w_query = jnp.dot(normed_in.T, grad_query_b, preferred_element_type=jnp.float32)
-    grad_w_key = jnp.dot(normed_in.T, grad_key_b, preferred_element_type=jnp.float32)
+    grad_w_query_key = jnp.dot(
+        normed_in.T,
+        jnp.concatenate([grad_query_b, grad_key_b], axis=1),
+        preferred_element_type=jnp.float32,
+    )
     grad_w_value = jnp.dot(normed_in.T, grad_value_b, preferred_element_type=jnp.float32)
     grad_normed = jnp.dot(grad_query_b, w_query.T, preferred_element_type=jnp.float32)
     grad_normed = grad_normed + jnp.dot(grad_key_b, w_key.T, preferred_element_type=jnp.float32)
@@ -500,28 +511,19 @@
         [grad_w_router, grad_gain_one[:, None], grad_gain_two[:, None]], axis=1
     )
     grad_small = jnp.pad(grad_small, ((0, 0), (0, small_width - grad_small.shape[1])))
-    blocks = sizes[0] * sizes[1]
-    own_a, own_b = scatter_rows(
+    own_qk, own_output, own_small, own_value = scatter_rows(
         sizes,
-        jnp.concatenate(
-            [
-                grad_w_query.astype(jnp.bfloat16),
-                grad_w_key.astype(jnp.bfloat16),
-                grad_small.astype(jnp.bfloat16),
-            ],
-            axis=1,
-        ).reshape(blocks, -1, full_a.shape[1]),
-        jnp.concatenate(
-            [grad_w_value.astype(jnp.bfloat16), grad_w_output.astype(jnp.bfloat16)], axis=1
-        ).reshape(blocks, -1, full_b.shape[1]),
-    )
-    own_small = own_a[:, query_width + key_width :]
+        grad_w_query_key.astype(jnp.bfloat16),
+        grad_w_output.astype(jnp.bfloat16),
+        grad_small.astype(jnp.bfloat16),
+        grad_w_value.astype(jnp.bfloat16),
+    )
     dense_grads = (
         own_small[:, experts_all],
-        own_a[:, :query_width],
-        own_a[:, query_width : query_width + key_width],
-        own_b[:, : value_weight.shape[1]],
-        own_b[:, value_weight.shape[1] :],
+        own_qk[:, :query_width],
+        own_qk[:, query_width:],
+        own_value,
+        own_output,
         own_small[:, experts_all + 1],
         own_small[:, :experts_all],
     )

time: 306 us -> 324 us (1.059)
  waiting for transfers between devices: 42.4 us -> 89.4 us
  blocking collectives: 25.3 us -> 0 us
  Pallas kernels: 105 us -> 85.6 us
  matrix products: 53.6 us -> 66.2 us
  other arithmetic: 26.4 us -> 30.7 us
    all_to_all x1 -> x0, blocking collectives: 25.3 us -> none  [shards(): lax.all_to_all(grad_send, 'dp', split_axis=0, concat_axis=0, tiled=True)]
    all_gather x1, waiting for transfers between devices: 0.01 us -> 20.2 us  [shards(): lax.all_gather(expert_down, 'fsdp', axis=1, tiled=True)]
    pallas_call x1, Pallas kernels: 58 us -> 39.7 us  [gather_rows(): pl.pallas_call(lambda *refs: gather_kernel(sizes, *refs), out_shape=tuple...]
    all_gather x1, waiting for transfers between devices: 0.02 us -> 11.8 us  [shards(): lax.all_gather(expert_gate, 'fsdp', axis=1, tiled=True)]
    all_to_all x1, waiting for transfers between devices: 17.9 us -> 29.6 us  [shards(): lax.all_to_all(jnp.concatenate([send_rows, grad_send], axis=1), 'dp', spl...]
    all_to_all x1, waiting for transfers between devices: 4.91 us -> 13.1 us  [shards(): lax.all_to_all(grad_rows_in.reshape(recv_rows.shape), 'dp', split_axis=0,...]
    concatenate x2 -> x0, local copies, waits for them, and re-layouts: 7.05 us -> none  [the longest x1 3.64 us: shards(): jnp.concatenate([grad_w_query.astype(jnp.bfloat16), grad_w_key.astype(jnp...]
    all_to_all x1, waiting for transfers between devices: 17.4 us -> 12.5 us  [shards(): lax.all_to_all(out_rows.reshape(recv_rows.shape), 'dp', split_axis=0, con...]
  transfers between devices with their start and end apart: 9 -> 9, of which waited for: 3 -> 5; matrix products, arithmetic and copies ran while one was open for 30% -> 23% of each run, Pallas kernels for 34% -> 14%
where the time goes in v2:
time: 324 us; the launch traced here: 323 us
  waiting for transfers between devices  89.4 us (28%)
  Pallas kernels  85.6 us (26%)
  matrix products  66.2 us (20%)
  other arithmetic  30.7 us (9%)
  local copies, waits for them, and re-layouts  20.2 us (6%)
  starting transfers between devices  15.9 us (5%)
  between operations  14.9 us (5%)
    pallas_call x1, Pallas kernels, scatter_rows(): pl.pallas_call(lambda *refs: scatter_kernel(sizes, width, *refs), out_sha...  45.9 us
    pallas_call x1, Pallas kernels, gather_rows(): pl.pallas_call(lambda *refs: gather_kernel(sizes, *refs), out_shape=tuple...  39.7 us
    all_to_all x1, waiting for transfers between devices, shards(): lax.all_to_all(jnp.concatenate([send_rows, grad_send], axis=1), 'dp', spl...  29.6 us
    all_gather x1, waiting for transfers between devices, shards(): lax.all_gather(expert_down, 'fsdp', axis=1, tiled=True)  20.2 us
    all_to_all x1, waiting for transfers between devices, shards(): lax.all_to_all(grad_rows_in.reshape(recv_rows.shape), 'dp', split_axis=0,...  13.1 us
    all_to_all x1, waiting for transfers between devices, shards(): lax.all_to_all(out_rows.reshape(recv_rows.shape), 'dp', split_axis=0, con...  12.5 us
    all_gather x1, waiting for transfers between devices, shards(): lax.all_gather(expert_gate, 'fsdp', axis=1, tiled=True)  11.8 us
    unnamed x95, local copies, waits for them, and re-layouts  7.02 us
  transfers between devices with their start and end apart: 9, of which 5 were waited for; matrix products, arithmetic and copies ran while one was open for 23% of the time, Pallas kernels for 14%

profile of v2, /device:TPU:0, one launch (start us, length us, event | category | flops | bytes accessed | tf_op | source)
XLA Modules:
  0.0 322.9 jit_solution(17244660166353488350)
XLA Ops:
  12.6 39.7 %gather_rows.1 = (bf16[32,32,1664]{2,1,0:T(8,128)(2,1)}, bf16[32,32,1536]{2,1,0:T(8,128)(2,1)}) custom-call(bf16[32,1664]{1,0:T(8,128)(2,1)} %pad_maximum_fusion.6.refs_0_, bf16[32,1536]{1,0:T(8,128)(2,1)} %pad_maximum_fusion.7.refs_1_), custom_call_target="tpu_custom_call" | custom-call | tf_op jit(solution)/shard_map/gather_rows/pallas_call | solution.py:234
  56.6 2.7 fusion.8
  66.6 2.8 fusion.25
  79.9 4.5 %all-to-all-start = ((bf16[16,48,1024]{2,1,0:T(8,128)(2,1)}), bf16[16,48,1024]{2,1,0:T(8,128)(2,1)}, u32[]{:S(2)}, u32[]{:S(2)}) async-start(bf16[16,48,1024]{2,1,0:T(8,128)(2,1)} %pad_maximum_fusion), calls=%async_computation | async-start | bytes 3145728 | tf_op jit(solution)/shard_map/all_to_all | solution.py:416
  86.6 29.6 %all-to-all-done = bf16[16,48,1024]{2,1,0:T(8,128)(2,1)} async-done(((bf16[16,48,1024]{2,1,0:T(8,128)(2,1)}), bf16[16,48,1024]{2,1,0:T(8,128)(2,1)}, u32[]{:S(2)}, u32[]{:S(2)}) %all-to-all-start) | async-done | bytes 1572896 | tf_op jit(solution)/shard_map/all_to_all | solution.py:416
  117.9 2.7 fusion.32
  120.6 11.8 %all-gather.4.cloned.1.call-done = bf16[1,1024,512]{2,1,0:T(8,128)(2,1)} async-done(((bf16[1,512,512]{2,1,0:T(8,128)(2,1)}), bf16[1,1024,512]{2,1,0:T(8,128)(2,1)}) %all-gather.4.cloned.1.call-update) | async-done | bytes 1048592 | tf_op jit(solution)/shard_map/all_gather | solution.py:371
  135.1 20.2 %all-gather.8.cloned.1.call-done = bf16[1,512,1024]{2,1,0:T(8,128)(2,1)} async-done(((bf16[1,256,1024]{2,1,0:T(8,128)(2,1)}), bf16[1,512,1024]{2,1,0:T(8,128)(2,1)}) %all-gather.8.cloned.1.call-update) | async-done | bytes 1048592 | tf_op jit(solution)/shard_map/all_gather | solution.py:373
  155.3 3.5 %multiply_convert_fusion.1 = (bf16[384,512]{1,0:T(8,128)(2,1)}, bf16[384,512]{1,0:T(8,128)(2,1)S(1)}, bf16[384,512]{1,0:T(8,128)(2,1)}) fusion(f32[384,512]{1,0:T(8,128)} %fusion.36, f32[384,512]{1,0:T(8,128)} %fusion.32, bf16[384,1024]{1,0:T(8,128)(2,1)S(1)} %bitcast.146, bf16[1,512,1024]{2,1,0:T(8,128)(2,1)} %all-gather.8.cloned.1.call-done), kind=kOutput, calls=%fused_computation.73 | convolution fusion | flops 405798912 | bytes 4587520 | tf_op jit(solution)/shard_map/dot_general | solution.py:112
  161.3 2.8 fusion.11
  164.1 2.8 convolution_convert_fusion.6
  166.9 5.6 %all-to-all-start.1 = ((bf16[16,24,1024]{2,1,0:T(8,128)(2,1)}), bf16[16,24,1024]{2,1,0:T(8,128)(2,1)S(1)}, u32[]{:S(2)}, u32[]{:S(2)}) async-start(bf16[16,24,1024]{2,1,0:T(8,128)(2,1)} %bitcast.164), calls=%async_computation.1 | async-start | bytes 1572864 | tf_op jit(solution)/shard_map/all_to_all | solution.py:426
  172.6 3.1 fusion.19
  178.8 12.5 %all-to-all-done.1 = bf16[16,24,1024]{2,1,0:T(8,128)(2,1)S(1)} async-done(((bf16[16,24,1024]{2,1,0:T(8,128)(2,1)}), bf16[16,24,1024]{2,1,0:T(8,128)(2,1)S(1)}, u32[]{:S(2)}, u32[]{:S(2)}) %all-to-all-start.1) | async-done | bytes 786464 | tf_op jit(solution)/shard_map/all_to_all | solution.py:426
  191.2 5.4 %all-to-all-start.2 = ((bf16[16,24,1024]{2,1,0:T(8,128)(2,1)}), bf16[16,24,1024]{2,1,0:T(8,128)(2,1)}, u32[]{:S(2)}, u32[]{:S(2)}) async-start(bf16[16,24,1024]{2,1,0:T(8,128)(2,1)} %bitcast.148), calls=%async_computation.2 | async-start | bytes 1572864 | tf_op jit(solution)/shard_map/all_to_all | solution.py:448
  196.9 2.7 fusion.12
  202.3 13.1 %all-to-all-done.2 = bf16[16,24,1024]{2,1,0:T(8,128)(2,1)} async-done(((bf16[16,24,1024]{2,1,0:T(8,128)(2,1)}), bf16[16,24,1024]{2,1,0:T(8,128)(2,1)}, u32[]{:S(2)}, u32[]{:S(2)}) %all-to-all-start.2) | async-done | bytes 786464 | tf_op jit(solution)/shard_map/all_to_all | solution.py:448
  220.0 5.4 %gather_fusion = bf16[1024,1024]{1,0:T(8,128)(2,1)} fusion(bf16[384,1024]{1,0:T(8,128)(2,1)S(1)} %bitcast.136, s32[1024]{0:T(1024)S(1)} %broadcast_clamp_fusion), kind=kCustom, calls=%fused_computation | custom fusion | bytes 4198400 | tf_op jit(solution)/shard_map/jit(_take)/gather | solution.py:437
  225.4 3.3 %multiply_reduce_fusion = f32[128,1024]{1,0:T(8,128)S(1)} fusion(bf16[1024,1024]{1,0:T(8,128)(2,1)} %gather_fusion, f32[128,8]{1,0:T(8,128)} %copy.75, pred[128,8]{1,0:T(8,128)(4,1)} %copy.76), kind=kLoop, calls=%fused_computation.3 | loop fusion | flops 4063232 | bytes 2626560 | tf_op jit(solution)/shard_map/reduce_sum | solution.py:438
  233.3 2.9 fusion.26
  238.5 3.4 %convolution_bitcast_fusion.4 = f32[128,8,64]{0,2,1:T(8,128)} fusion(f32[8,2,128,128]{2,3,1,0:T(8,128)} %fusion.19, f32[8,2,128,128]{2,3,1,0:T(8,128)} %convolution_bitcast_fusion, bf16[128,8,2,32]{0,3,2,1:T(8,128)(2,1)} %get-tuple-element.80, bf16[128,8,2,32]{0,3,2,1:T(8,128)(2,1)} %get-tuple-element.79), kind=kOutput, calls=%fused_computation.48 | convolution fusion | flops 35391616 | bytes 2621440 | tf_op jit(solution)/shard_map/kgij,ikgd->jkd/dot_general | solution.py:477
  241.9 3.5 %convolution_bitcast_fusion.1 = f32[128,8,2,64]{0,3,2,1:T(8,128)} fusion(f32[8,2,128,128]{2,3,1,0:T(8,128)} %fusion.19, f32[8,2,128,128]{2,3,1,0:T(8,128)} %convolution_bitcast_fusion, bf16[128,8,32]{0,2,1:T(8,128)(2,1)} %get-tuple-element.86, bf16[128,8,32]{0,2,1:T(8,128)(2,1)} %get-tuple-element.85), kind=kOutput, calls=%fused_computation.41 | convolution fusion | flops 35129472 | bytes 2752512 | tf_op jit(solution)/shard_map/kgij,jkd->ikgd/dot_general | solution.py:474
  256.1 2.7 convolution_convert_fusion
  258.8 45.9 %scatter_rows.1 = (f32[32,1536]{1,0:T(8,128)S(1)}, f32[32,1024]{1,0:T(8,128)S(1)}, f32[32,128]{1,0:T(8,128)S(1)}, f32[32,512]{1,0:T(8,128)S(1)}) custom-call(bf16[32,32,1536]{2,1,0:T(8,128)(2,1)} %bitcast.141, bf16[32,32,1024]{2,1,0:T(8,128)(2,1)S(1)} %bitcast.132, bf16[32,32,128]{2,1,0:T(8,128)(2,1)S(1)} %bitcast.134, bf16[32,32,512]{2,1,0:T(8,128)(2,1)S(1)} %bitcast.133), custom_call_target="tpu_custom_call" | custom-call | tf_op jit(solution)/shard_map/scatter_rows/pallas_call | solution.py:316
  (186 shorter events, 75.3 us)
Async XLA Ops:
  7.2 47.3 %copy-start = (bf16[128,1024]{1,0:T(8,128)(2,1)S(1)}, bf16[128,1024]{1,0:T(8,128)(2,1)}, u32[]{:S(2)}) copy-start(bf16[128,1024]{1,0:T(8,128)(2,1)} %param.14) | copy-start | bytes 786436
  54.5 7.7 %copy-start.26 = (f32[1024,1]{0,1:T(1,128)}, f32[1024,1]{0,1:T(1,128)S(1)}, u32[]{:S(2)}) copy-start(f32[1024,1]{0,1:T(1,128)S(1)} %copy.98) | copy-start | bytes 12292
  54.7 7.5 %copy-start.38 = (f32[128]{0:T(128)}, f32[128]{0:T(128)S(1)}, u32[]{:S(2)}) copy-start(f32[128]{0:T(128)S(1)} %add_rsqrt_fusion.1) | copy-start | bytes 1540
  56.5 5.7 %copy-start.1 = (bf16[32,32,1536]{2,1,0:T(8,128)(2,1)S(1)}, bf16[32,32,1536]{2,1,0:T(8,128)(2,1)}, u32[]{:S(2)}) copy-start(bf16[32,32,1536]{2,1,0:T(8,128)(2,1)} %get-tuple-element.19) | copy-start | bytes 9437188
  71.7 6.4 %copy-start.13 = (bf16[128,1024]{1,0:T(8,128)(2,1)S(1)}, bf16[128,1024]{1,0:T(8,128)(2,1)}, u32[]{:S(2)}) copy-start(bf16[128,1024]{1,0:T(8,128)(2,1)} %param.17) | copy-start | bytes 786436
  73.7 4.8 %copy-start.28 = (f32[128,16]{0,1:T(8,128)}, f32[128,16]{0,1:T(8,128)S(1)}, u32[]{:S(2)}) copy-start(f32[128,16]{0,1:T(8,128)S(1)} %convert_reduce_fusion) | copy-start | bytes 24580
  79.9 36.4 %all-to-all-start = ((bf16[16,48,1024]{2,1,0:T(8,128)(2,1)}), bf16[16,48,1024]{2,1,0:T(8,128)(2,1)}, u32[]{:S(2)}, u32[]{:S(2)}) async-start(bf16[16,48,1024]{2,1,0:T(8,128)(2,1)} %pad_maximum_fusion), calls=%async_computation | async-start | bytes 3145728 | tf_op jit(solution)/shard_map/all_to_all | solution.py:416
  84.3 33.5 %all-gather.6.cloned.1.call-start = ((), (), s32[]{:S(2)}) async-start(), calls=%async_computation.7 | async-start | bytes 1572864 | tf_op jit(solution)/shard_map/all_gather | solution.py:372
  85.1 47.3 %all-gather.4.cloned.1.call-start = ((), (), s32[]{:S(2)}) async-start(), calls=%async_computation.6 | async-start | bytes 1572864 | tf_op jit(solution)/shard_map/all_gather | solution.py:371
  85.8 69.4 %all-gather.8.cloned.1.call-start = ((), (), s32[]{:S(2)}) async-start(), calls=%async_computation.8 | async-start | bytes 1572864 | tf_op jit(solution)/shard_map/all_gather | solution.py:373
  86.6 221.8 %reduce-scatter.4.cloned.1.call-start = ((), (), s32[]{:S(2)}) async-start(), calls=%async_computation.9 | async-start | bytes 1572864 | tf_op jit(solution)/shard_map/reduce_scatter | solution.py:531
  161.2 149.3 %reduce-scatter.6.cloned.1.call-start = ((), (), s32[]{:S(2)}) async-start(), calls=%async_computation.10 | async-start | bytes 1572864 | tf_op jit(solution)/shard_map/reduce_scatter | solution.py:534
  166.9 24.3 %all-to-all-start.1 = ((bf16[16,24,1024]{2,1,0:T(8,128)(2,1)}), bf16[16,24,1024]{2,1,0:T(8,128)(2,1)S(1)}, u32[]{:S(2)}, u32[]{:S(2)}) async-start(bf16[16,24,1024]{2,1,0:T(8,128)(2,1)} %bitcast.164), calls=%async_computation.1 | async-start | bytes 1572864 | tf_op jit(solution)/shard_map/all_to_all | solution.py:426
  172.6 4.7 %copy-start.9 = (bf16[1,1024,512]{2,1,0:T(8,128)(2,1)S(1)}, bf16[1,1024,512]{2,1,0:T(8,128)(2,1)}, u32[]{:S(2)}) copy-start(bf16[1,1024,512]{2,1,0:T(8,128)(2,1)} %all-gather.6.cloned.1.call-done) | copy-start | bytes 3145732
  172.6 4.7 %copy-start.11 = (bf16[384,512]{1,0:T(8,128)(2,1)S(1)}, bf16[384,512]{1,0:T(8,128)(2,1)}, u32[]{:S(2)}) copy-start(bf16[384,512]{1,0:T(8,128)(2,1)} %get-tuple-element.72) | copy-start | bytes 1179652
  191.2 24.2 %all-to-all-start.2 = ((bf16[16,24,1024]{2,1,0:T(8,128)(2,1)}), bf16[16,24,1024]{2,1,0:T(8,128)(2,1)}, u32[]{:S(2)}, u32[]{:S(2)}) async-start(bf16[16,24,1024]{2,1,0:T(8,128)(2,1)} %bitcast.148), calls=%async_computation.2 | async-start | bytes 1572864 | tf_op jit(solution)/shard_map/all_to_all | solution.py:448
  196.7 116.0 %reduce-scatter.8.cloned.1.call-start = ((), (), s32[]{:S(2)}) async-start(), calls=%async_computation.11 | async-start | bytes 1572864 | tf_op jit(solution)/shard_map/reduce_scatter | solution.py:537
  199.7 17.2 %copy-start.3 = (f32[128,1024]{1,0:T(8,128)S(1)}, f32[128,1024]{1,0:T(8,128)}, u32[]{:S(2)}) copy-start(f32[128,1024]{1,0:T(8,128)} %get-tuple-element.94) | copy-start | bytes 1572868
  199.7 17.2 %copy-start.31 = (f32[1024,1]{0,1:T(1,128)S(1)}, f32[1024,1]{0,1:T(1,128)}, u32[]{:S(2)}) copy-start(f32[1024,1]{0,1:T(1,128)} %copy-done.30) | copy-start | bytes 12292
  199.7 17.2 %copy-start.41 = (f32[128]{0:T(128)S(1)}, f32[128]{0:T(128)}, u32[]{:S(2)}) copy-start(f32[128]{0:T(128)} %copy-done.40) | copy-start | bytes 1540
  200.6 19.4 %copy-start.32 = (bf16[128,16]{0,1:T(8,128)(2,1)}, bf16[128,16]{0,1:T(8,128)(2,1)S(1)}, u32[]{:S(2)}) copy-start(bf16[128,16]{0,1:T(8,128)(2,1)S(1)} %get-tuple-element.87) | copy-start | bytes 12292
  225.4 6.4 %copy-start.2 = (bf16[32,32,1536]{2,1,0:T(8,128)(2,1)S(1)}, bf16[32,32,1536]{2,1,0:T(8,128)(2,1)}, u32[]{:S(2)}) copy-start(bf16[32,32,1536]{2,1,0:T(8,128)(2,1)} %get-tuple-element.19) | copy-start | bytes 9437188
  238.5 6.9 %copy-start.19 = (f32[128,32]{0,1:T(8,128)S(1)}, f32[128,32]{0,1:T(8,128)}, u32[]{:S(2)}) copy-start(f32[128,32]{0,1:T(8,128)} %copy-done.18) | copy-start | bytes 49156
  258.8 48.6 %copy-start.10 = (f32[128,1024]{1,0:T(8,128)S(1)}, f32[128,1024]{1,0:T(8,128)}, u32[]{:S(2)}) copy-start(f32[128,1024]{1,0:T(8,128)} %get-tuple-element.100) | copy-start | bytes 1572868
  (29 other events, 68.4 us)
Sparse Core Ops, SparseCore 0:
  86.7 22.7 all-gather.5
  111.1 21.2 all-gather.3
  133.9 21.2 all-gather.7
  161.4 20.3 reduce-scatter.3
  183.9 20.3 reduce-scatter.5
  206.4 20.3 reduce-scatter.7
